TPU v7x, 32 devices: a whole 2x2x4 slice. The times are simulated.
32 devices in a mesh: facet: 4 (over z), pol: 4 (over y, x), tm: 2 (over core).
Axes of the slice: x: 2, y: 2, z: 4, core: 2. Of those that a mesh axis runs over, the one named last changes fastest.
Arguments:
- tile_spectral_lines: bfloat16 [64, 4, 2, 64, 4096], P('facet', 'pol', None, 'tm'), may hold values from -6 to 6
- taper_leading_axis: bfloat16 [4, 2, 128, 512], P('facet', 'tm'), may hold values from -0.25 to 0.25
- taper_trailing_axis: bfloat16 [4, 2, 128, 512], P('facet', 'tm'), may hold values from -0.25 to 0.25
- depth_layer_factors: bfloat16 [4, 2, 2, 128], P('facet', 'tm'), may hold values from -4 to 4
- measured_correlations: float32 [4, 8, 2, 128], P('facet', None, 'tm', 'pol'), may hold values from -6 to 6
- visibility_groups_table: int32 [4, 2, 3, 8], P('facet', 'tm'), may hold values from 0 to 130815, as said below
- antenna_links: int32 [2, 130816], replicated, may hold values from 0 to 511, as said below
- complex_receiver_factors: float32 [256, 4, 512], replicated, may hold values from -5 to 5
Outputs:
- residual: float32 [4, 8, 2, 128], P('facet', None, 'tm', 'pol')
- gain_grad: float32 [512, 1024], P(('facet', 'pol', 'tm'))
Inputs may be any that keep to these rules, and one draw needn't show every extreme that they name: `visibility_groups_table`: for each subgrid and owner, every block has a channel below 256, a count of 1 or more, and baselines offset to offset + count - 1 below 130816; the counts of one owner sum to at most 128, and some owner reaches 128 in every draw. `antenna_links`: each baseline joins two different stations.
All inputs are finite; a program needn't handle non-finite values.
Results may differ from a plain program's by a relative error of at most 0.012.
Values may be sent and summed in bfloat16 or wider, within the bound.
A program may use at most 192 MiB of HBM per device.

v0:
```python
import functools
import math

import jax
import jax.numpy as jnp
import numpy as np
from jax import lax
from jax.experimental import pallas as pl
from jax.experimental.pallas import tpu as pltpu
from jax.sharding import PartitionSpec as P

FGRID = 8
FS = 4096
MC = 64
SG = 512
NPOL = 4
NW = 2
NCH = 256
NST = 512
CHUNK = 1024

w_chirp = 0.37
grad_scale = 0.1


def unit_angles(left, right, length):
    product = np.outer(np.arange(left), np.arange(right)) % length
    return 2.0 * math.pi * product / length


def fourier_factors(subgrids):
    spread = FS // MC
    alpha = unit_angles(FS // spread, MC, MC)
    p = np.concatenate([np.cos(alpha), -np.sin(alpha)], axis=1) / math.sqrt(FS)
    q = np.concatenate([-np.sin(alpha), -np.cos(alpha)], axis=1) / math.sqrt(FS)
    beta = unit_angles(spread, subgrids * MC, FS).reshape(spread, subgrids, 1, MC)
    beta = np.broadcast_to(beta, (spread, subgrids, 2, MC)).reshape(spread, subgrids * 2 * MC)
    tile = lambda t: np.tile(t, (1, subgrids)).astype(np.float32)
    return (
        tile(p),
        tile(q),
        np.cos(beta).astype(np.float32),
        np.sin(beta).astype(np.float32),
    )


def fetch_lookups(block_ref, links_ref, gain_ref, window, channel_gain, window_sem, gain_sem):
    blocks, _, span = window.shape
    copies = []
    for b in range(blocks):
        first = jnp.minimum(block_ref[1, b] // 128 * 128, links_ref.shape[1] - span)
        first = pl.multiple_of(first, 128)
        copies.append(
            pltpu.make_async_copy(
                links_ref.at[:, pl.ds(first, span)], window.at[b], window_sem.at[b]
            )
        )
        copies.append(
            pltpu.make_async_copy(
                gain_ref.at[block_ref[0, b]], channel_gain.at[b], gain_sem.at[b]
            )
        )
    return copies


def use_lookups(block_ref, links_ref, window, channel_gain, gains_ref, idents_ref):
    blocks, _, span = window.shape
    slots = idents_ref.shape[1]
    lane = lax.broadcasted_iota(jnp.int32, (1, slots), 1)
    place = lax.broadcasted_iota(jnp.int32, (span, slots), 0)
    lane_tall = lax.broadcasted_iota(jnp.int32, (span, slots), 1)
    begin = jnp.int32(0)
    member, picks = [], []
    channel = jnp.zeros((1, slots), jnp.float32)
    alive = jnp.zeros((1, slots), jnp.float32)
    for b in range(blocks):
        offset, amount = block_ref[1, b], block_ref[2, b]
        first = jnp.minimum(offset // 128 * 128, links_ref.shape[1] - span)
        inside = jnp.where((lane >= begin) & (lane < begin + amount), 1.0, 0.0)
        member.append(inside)
        alive += inside
        channel += inside * block_ref[0, b].astype(jnp.float32)
        hit = place == lane_tall + (offset - first - begin)
        picks.append((jnp.where(hit, 1.0, 0.0) * inside).astype(jnp.bfloat16))
        begin = begin + amount
    links = jnp.concatenate([window[b] for b in range(blocks)], axis=1)
    upper = links // 16
    lower = links - 16 * upper
    pieces = jnp.concatenate([upper, lower], axis=0).astype(jnp.float32).astype(jnp.bfloat16)
    found = jnp.dot(
        pieces, jnp.concatenate(picks, axis=0), preferred_element_type=jnp.float32
    )
    stations = 16.0 * found[0:2] + found[2:4]
    table = channel_gain[...].reshape(blocks * 4, channel_gain.shape[2])
    high = table.astype(jnp.bfloat16)
    rest = table - high.astype(jnp.float32)
    middle = rest.astype(jnp.bfloat16)
    low = (rest - middle.astype(jnp.float32)).astype(jnp.bfloat16)
    names = lax.broadcasted_iota(jnp.int32, (table.shape[1], 1), 0).astype(jnp.float32)
    for side in range(2):
        pick = jnp.where(names == stations[side : side + 1], 1.0, 0.0).astype(jnp.bfloat16)
        rows = (
            jnp.dot(high, pick, preferred_element_type=jnp.float32)
            + jnp.dot(middle, pick, preferred_element_type=jnp.float32)
            + jnp.dot(low, pick, preferred_element_type=jnp.float32)
        )
        chosen = member[0] * rows[0:4]
        for b in range(1, blocks):
            chosen = chosen + member[b] * rows[4 * b : 4 * b + 4]
        gains_ref[4 * side : 4 * side + 4, :] = chosen
    idents_ref[0:2, :] = stations
    idents_ref[2:3, :] = channel
    idents_ref[3:4, :] = alive
    idents_ref[4:8, :] = jnp.zeros((4, slots), jnp.float32)


def fourier_kernel(
    block_ref,
    links_ref,
    gain_ref,
    p_ref,
    q_ref,
    c_ref,
    s_ref,
    x_ref,
    o_ref,
    gains_ref,
    idents_ref,
    table,
    total,
    window,
    channel_gain,
    window_sem,
    gain_sem,
):
    step = pl.program_id(0)
    copies = fetch_lookups(
        block_ref, links_ref, gain_ref, window, channel_gain, window_sem, gain_sem
    )

    @pl.when(step == 0)
    def _():
        for copy in copies:
            copy.start()

    @pl.when(step == pl.num_programs(0) - 1)
    def _():
        for copy in copies:
            copy.wait()
        use_lookups(block_ref, links_ref, window, channel_gain, gains_ref, idents_ref)

    facets, _, rows, chunk = x_ref.shape
    subgrids = o_ref.shape[0]
    spread = c_ref.shape[0]
    cosine, sine = c_ref[...], s_ref[...]
    for part in range(chunk // spread):
        lead = p_ref[part : part + 1, :]
        other = q_ref[part : part + 1, :]
        table[part * spread : (part + 1) * spread, :] = (lead * cosine + other * sine).astype(
            jnp.bfloat16
        )
    x = x_ref[...].reshape(facets * 2 * rows, chunk)
    product = jnp.dot(x, table[...], preferred_element_type=jnp.float32)

    @pl.when(step == 0)
    def _():
        total[...] = product

    @pl.when(step > 0)
    def _():
        total[...] += product

    @pl.when(step == pl.num_programs(0) - 1)
    def _():
        lane = lax.broadcasted_iota(jnp.int32, (rows, 2 * MC), 1)
        sign = jnp.where(lane < MC, -1.0, 1.0)
        packed = o_ref.shape[3] // (2 * MC)
        for f in range(facets):
            for s in range(subgrids):
                cut = slice(s * 2 * MC, (s + 1) * 2 * MC)
                first = total[2 * f * rows : (2 * f + 1) * rows, cut]
                second = total[(2 * f + 1) * rows : (2 * f + 2) * rows, cut]
                value = first + sign * pltpu.roll(second, MC, 1)
                j = f % packed
                o_ref[s, f // packed, :, j * 2 * MC : (j + 1) * 2 * MC] = value.astype(jnp.bfloat16)


def fourier(x, subgrids, slots, block_table, links, station_gains):
    facets, _, rows, length = x.shape
    width = subgrids * 2 * MC
    spread = FS // MC
    packed = FGRID if facets % FGRID == 0 else 1
    per_step = CHUNK // spread
    blocks = block_table.shape[1]
    span = slots + 128
    in_place = lambda array: pltpu.with_memory_space_constraint(array, pltpu.HBM)
    factors = [in_place(jnp.asarray(t)) for t in fourier_factors(subgrids)]
    out = (subgrids, facets // packed, rows, packed * 2 * MC)
    return pl.pallas_call(
        fourier_kernel,
        out_shape=(
            jax.ShapeDtypeStruct(out, jnp.bfloat16),
            jax.ShapeDtypeStruct((8, slots), jnp.float32),
            jax.ShapeDtypeStruct((8, slots), jnp.float32),
        ),
        grid=(length // CHUNK,),
        in_specs=[
            pl.BlockSpec(memory_space=pltpu.SMEM),
            pl.BlockSpec(memory_space=pltpu.HBM),
            pl.BlockSpec(memory_space=pltpu.HBM),
            pl.BlockSpec((per_step, width), lambda g: (g, 0)),
            pl.BlockSpec((per_step, width), lambda g: (g, 0)),
            pl.BlockSpec((spread, width), lambda g: (0, 0)),
            pl.BlockSpec((spread, width), lambda g: (0, 0)),
            pl.BlockSpec((facets, 2, rows, CHUNK), lambda g: (0, 0, 0, g)),
        ],
        out_specs=(
            pl.BlockSpec(out, lambda g: (0, 0, 0, 0)),
            pl.BlockSpec((8, slots), lambda g: (0, 0)),
            pl.BlockSpec((8, slots), lambda g: (0, 0)),
        ),
        scratch_shapes=[
            pltpu.VMEM((CHUNK, width), jnp.bfloat16),
            pltpu.VMEM((facets * 2 * rows, width), jnp.float32),
            pltpu.VMEM((blocks, 2, span), jnp.int32),
            pltpu.VMEM((blocks, 4, NST), jnp.float32),
            pltpu.SemaphoreType.DMA((blocks,)),
            pltpu.SemaphoreType.DMA((blocks,)),
        ],
        compiler_params=pltpu.CompilerParams(
            dimension_semantics=("arbitrary",), vmem_limit_bytes=48 << 20
        ),
    )(
        block_table,
        in_place(links),
        in_place(station_gains),
        *factors,
        x,
    )


def subgrid_tables():
    angle = unit_angles(SG, SG, SG)
    re = np.cos(angle) / math.sqrt(SG)
    im = np.sin(angle) / math.sqrt(SG)
    blocks = lambda t: t.reshape(SG, FGRID, MC)
    second = np.stack([blocks(re), -blocks(im)], axis=2).reshape(SG, 2 * SG)
    return [t.astype(jnp.bfloat16) for t in (re, im, second)]


def chirp_line():
    offset = np.arange(SG) - SG // 2
    angle = 2.0 * math.pi * w_chirp * (offset * offset) / float(SG * SG)
    return np.cos(angle).astype(np.float32), np.sin(angle).astype(np.float32)


def model_terms(pred, observed, first, second, alive):
    residual, lead, trail = [], [], []
    for p in range(NPOL):
        f1, f2 = p // 2, p % 2
        pred_re, pred_im = pred[p]
        first_re, first_im = first[2 * f1], first[2 * f1 + 1]
        second_re, second_im = second[2 * f2], second[2 * f2 + 1]
        both_re = first_re * second_re + first_im * second_im
        both_im = first_im * second_re - first_re * second_im
        resid_re = alive * (observed[2 * p] - (both_re * pred_re - both_im * pred_im))
        resid_im = alive * (observed[2 * p + 1] - (both_re * pred_im + both_im * pred_re))
        cross_re = second_re * pred_re + second_im * pred_im
        cross_im = second_im * pred_re - second_re * pred_im
        along_re = first_re * pred_re - first_im * pred_im
        along_im = first_re * pred_im + first_im * pred_re
        residual += [resid_re, resid_im]
        lead.append(
            (-(resid_re * cross_re - resid_im * cross_im), -(resid_re * cross_im + resid_im * cross_re))
        )
        trail.append(
            (-(resid_re * along_re + resid_im * along_im), -(resid_re * along_im - resid_im * along_re))
        )
    leading = [lead[2 * f][r] + lead[2 * f + 1][r] for f in range(2) for r in range(2)]
    trailing = [trail[f][r] + trail[f + 2][r] for f in range(2) for r in range(2)]
    return residual, leading, trailing


def nt_dot(left, right, **kw):
    return lax.dot_general(
        left, right, (((1,), (1,)), ((), ())), preferred_element_type=jnp.float32, **kw
    )


def chirped_rows(taper, chirp_ref):
    wide = taper.astype(jnp.float32)
    return jnp.concatenate(
        [
            taper,
            (wide * chirp_ref[0:1, :]).astype(jnp.bfloat16),
            (wide * chirp_ref[1:2, :]).astype(jnp.bfloat16),
        ],
        axis=0,
    )


def predict_kernel(
    sizes,
    contrib_ref,
    lead_ref,
    trail_ref,
    depth_ref,
    observed_ref,
    gains_ref,
    idents_ref,
    table_re_ref,
    table_im_ref,
    second_ref,
    chirp_ref,
    residual_ref,
    grad_ref,
    got,
    lines,
    tapers,
    right,
    left,
    part_out,
    part_in,
    observed_out,
    observed_in,
    record_out,
    record_in,
    got_send,
    got_recv,
    taper_send,
    taper_recv,
    observed_send,
    observed_recv,
    part_send,
    part_recv,
    record_send,
    record_recv,
):
    subgrids, pols, owners = sizes
    z, p, t = lax.axis_index("facet"), lax.axis_index("pol"), lax.axis_index("tm")
    slots = lead_ref.shape[0]
    _, groups, rows, width = contrib_ref.shape
    mesh_id = pl.DeviceIdType.MESH

    def remote(src, dst, send, recv, peer):
        return pltpu.make_async_remote_copy(
            src_ref=src,
            dst_ref=dst,
            send_sem=send,
            recv_sem=recv,
            device_id=peer,
            device_id_type=mesh_id,
        )

    across_total = subgrids * owners
    plane_total = pols * owners
    across = z * owners + t
    plane = p * owners + t

    def across_peer(d):
        other = lax.rem(across + d, across_total)
        return other, (other // owners, p, lax.rem(other, owners))

    def plane_peer(d):
        other = lax.rem(plane + d, plane_total)
        return other, (z, other // owners, lax.rem(other, owners))

    barrier = pltpu.get_barrier_semaphore()
    for d in range(1, across_total):
        pl.semaphore_signal(barrier, inc=1, device_id=across_peer(d)[1], device_id_type=mesh_id)
    for d in range(1, pols):
        q = lax.rem(p + d, pols)
        for o in range(owners):
            pl.semaphore_signal(barrier, inc=1, device_id=(z, q, o), device_id_type=mesh_id)
    pl.semaphore_wait(barrier, across_total - 1 + (pols - 1) * owners)

    quarter = observed_ref.shape[1]
    place = lax.broadcasted_iota(jnp.int32, (2 * NPOL, slots), 1)
    observed_out[...] = jnp.where(
        (place >= p * quarter) & (place < (p + 1) * quarter),
        jnp.concatenate([observed_ref[...]] * pols, axis=1),
        0.0,
    )
    copies = []
    for d in sorted(range(1, subgrids), key=lambda d: -min(d, subgrids - d)):
        other = lax.rem(z + d, subgrids)
        copies.append(
            remote(contrib_ref.at[other], got.at[z], got_send.at[d], got_recv.at[d], (other, p, t))
        )
    partner = lax.rem(t + 1, owners)
    taper_copies = [
        remote(ref, tapers.at[t, k], taper_send.at[k], taper_recv.at[k], (z, p, partner))
        for k, ref in enumerate((trail_ref, lead_ref))
    ]
    observed_copies = []
    for d in range(1, pols):
        q = lax.rem(p + d, pols)
        observed_copies.append(
            remote(
                observed_out, observed_in.at[p], observed_send.at[d], observed_recv.at[d], (z, q, t)
            )
        )
    for copy in copies + taper_copies + observed_copies:
        copy.start()

    table_re = jnp.concatenate([table_re_ref[i, t] for i in range(FGRID)], axis=0)
    table_im = jnp.concatenate([table_im_ref[i, t] for i in range(FGRID)], axis=0)

    turn = jnp.where(
        lax.broadcasted_iota(jnp.int32, (3 * slots, 2 * MC), 1) < MC, -1.0, 1.0
    )

    def prepare(owner, trail, lead):
        trail3 = chirped_rows(trail, chirp_ref)
        a = jnp.dot(trail3, second_ref[...], preferred_element_type=jnp.float32)
        b = jnp.concatenate(
            [
                turn * pltpu.roll(a[:, j * 2 * MC : (j + 1) * 2 * MC], MC, 1)
                for j in range(a.shape[1] // (2 * MC))
            ],
            axis=1,
        )
        n0, n1, n2 = slice(0, slots), slice(slots, 2 * slots), slice(2 * slots, 3 * slots)
        right[owner, 0:slots, :] = a[n0].astype(jnp.bfloat16)
        right[owner, slots : 2 * slots, :] = (a[n1] - b[n2]).astype(jnp.bfloat16)
        right[owner, 2 * slots : 3 * slots, :] = b[n0].astype(jnp.bfloat16)
        right[owner, 3 * slots : 4 * slots, :] = (b[n1] + a[n2]).astype(jnp.bfloat16)
        lead3 = chirped_rows(lead, chirp_ref)
        u = nt_dot(table_re, lead3)
        v = nt_dot(table_im, lead3)
        left[owner, 0] = u[:, n0]
        left[owner, 1] = v[:, n0]
        left[owner, 2] = u[:, n1] - v[:, n2]
        left[owner, 3] = u[:, n2] + v[:, n1]

    prepare(t, trail_ref[...], lead_ref[...])
    got[z] = contrib_ref[z]
    for copy in taper_copies:
        copy.wait()
    prepare(partner, tapers[partner, 0], tapers[partner, 1])
    for copy in copies:
        copy.wait()
    if width == 2 * SG:
        whole = got[...].reshape(subgrids * groups * rows, width)
    else:
        for f in range(subgrids * groups):
            i, j = f // FGRID, f % FGRID
            lines[i * rows : (i + 1) * rows, j * 2 * MC : (j + 1) * 2 * MC] = got[
                f // groups, f % groups
            ]
        whole = lines[...]
    for o in range(owners):
        spread = nt_dot(whole, right[o])
        for w in range(NW):
            g_re = spread[:, w * slots : (w + 1) * slots]
            g_im = spread[:, (NW + w) * slots : (NW + w + 1) * slots]
            l_re, l_im = left[o, 2 * w], left[o, 2 * w + 1]
            part_out[o, 2 * w : 2 * w + 1, :] = jnp.sum(l_re * g_re - l_im * g_im, axis=0, keepdims=True)
            part_out[o, 2 * w + 1 : 2 * w + 2, :] = jnp.sum(
                l_re * g_im + l_im * g_re, axis=0, keepdims=True
            )
        part_out[o, 2 * NW :, :] = jnp.zeros((8 - 2 * NW, slots), jnp.float32)

    part_copies = []
    for d in range(1, plane_total):
        other, peer = plane_peer(d)
        part_copies.append(
            remote(
                part_out.at[lax.rem(other, owners)],
                part_in.at[plane],
                part_send.at[d],
                part_recv.at[d],
                peer,
            )
        )
    for copy in part_copies:
        copy.start()
    part_in[plane] = part_out[t]
    observed_in[p] = observed_out[...]
    for copy in observed_copies:
        copy.wait()
    observed = observed_in[0]
    for q in range(1, pols):
        observed = observed + observed_in[q]
    depth = depth_ref[...].astype(jnp.float32)
    for copy in part_copies:
        copy.wait()

    pred = []
    per_pol = part_in.shape[0] // NPOL
    for q in range(NPOL):
        block = part_in[q * per_pol]
        for o in range(1, per_pol):
            block = block + part_in[q * per_pol + o]
        pred.append(
            tuple(
                sum(depth[w : w + 1] * block[2 * w + c : 2 * w + c + 1] for w in range(NW))
                for c in range(2)
            )
        )
    gains = gains_ref[...]
    idents = idents_ref[...]
    residual, leading, trailing = model_terms(
        pred,
        [observed[k : k + 1] for k in range(2 * NPOL)],
        [gains[k : k + 1] for k in range(4)],
        [gains[4 + k : 5 + k] for k in range(4)],
        idents[3:4],
    )
    for k in range(3):
        record_out[k : k + 1, :] = idents[k : k + 1]
    for k in range(4):
        record_out[3 + k : 4 + k, :] = leading[k]
        record_out[7 + k : 8 + k, :] = trailing[k]
    record_out[11:, :] = jnp.zeros((5, slots), jnp.float32)
    record_copies = []
    for d in range(1, across_total):
        other, peer = across_peer(d)
        record_copies.append(
            remote(record_out, record_in.at[across], record_send.at[d], record_recv.at[d], peer)
        )
    for copy in record_copies:
        copy.start()
    record_in[across] = record_out[...]
    rest = jnp.concatenate(residual, axis=0)
    own_rest = jnp.zeros((2 * NPOL, quarter), jnp.float32)
    for q in range(pols):
        own_rest = jnp.where(p == q, rest[:, q * quarter : (q + 1) * quarter], own_rest)
    residual_ref[...] = own_rest
    for copy in record_copies:
        copy.wait()

    piece = jnp.concatenate([record_in[d] for d in range(across_total)], axis=1)
    own_count = grad_ref.shape[1]
    index = (z * pols + p) * owners + t
    mine = (index * own_count + lax.broadcasted_iota(jnp.int32, (own_count, 1), 0)).astype(
        jnp.float32
    )
    match_first = mine == piece[0:1]
    match_second = mine == piece[1:2]
    weighted = jnp.concatenate(
        [
            jnp.where(match_first, piece[3 + k : 4 + k], 0.0)
            + jnp.where(match_second, piece[7 + k : 8 + k], 0.0)
            for k in range(4)
        ],
        axis=0,
    )
    high = weighted.astype(jnp.bfloat16)
    low = (weighted - high.astype(jnp.float32)).astype(jnp.bfloat16)
    channel_ids = lax.broadcasted_iota(jnp.int32, (NCH, 1), 0).astype(jnp.float32)
    onehot = jnp.where(channel_ids == piece[2:3], 1.0, 0.0).astype(jnp.bfloat16)
    summed = nt_dot(high, onehot) + nt_dot(low, onehot)
    for k in range(4):
        grad_ref[k] = grad_scale * summed[k * own_count : (k + 1) * own_count]


def predict(sizes, own_count, *operands):
    subgrids, pols, owners = sizes
    contrib, lead = operands[0], operands[1]
    _, groups, rows, width = contrib.shape
    slots = lead.shape[0]
    vmem = pl.BlockSpec(memory_space=pltpu.VMEM)
    dma = lambda n: pltpu.SemaphoreType.DMA((n,))
    across_total, plane_total = subgrids * owners, pols * owners
    return pl.pallas_call(
        functools.partial(predict_kernel, sizes),
        out_shape=(
            jax.ShapeDtypeStruct((2 * NPOL, slots // pols), jnp.float32),
            jax.ShapeDtypeStruct((4, own_count, NCH), jnp.float32),
        ),
        in_specs=[vmem] * len(operands),
        out_specs=(vmem, vmem),
        scratch_shapes=[
            pltpu.VMEM(contrib.shape, jnp.bfloat16),
            pltpu.VMEM((FGRID * rows, 2 * SG), jnp.bfloat16),
            pltpu.VMEM((owners, 2, slots, SG), jnp.bfloat16),
            pltpu.VMEM((owners, 2 * NW * slots, 2 * SG), jnp.bfloat16),
            pltpu.VMEM((owners, 4, FGRID * rows, slots), jnp.float32),
            pltpu.VMEM((owners, 8, slots), jnp.float32),
            pltpu.VMEM((plane_total, 8, slots), jnp.float32),
            pltpu.VMEM((8, slots), jnp.float32),
            pltpu.VMEM((pols, 8, slots), jnp.float32),
            pltpu.VMEM((16, slots), jnp.float32),
            pltpu.VMEM((across_total, 16, slots), jnp.float32),
            dma(subgrids),
            dma(subgrids),
            dma(2),
            dma(2),
            dma(pols),
            dma(pols),
            dma(plane_total),
            dma(plane_total),
            dma(across_total),
            dma(across_total),
        ],
        compiler_params=pltpu.CompilerParams(
            collective_id=0, has_side_effects=True, vmem_limit_bytes=48 << 20
        ),
    )(*operands)


def on_device(
    tile_spectral_lines,
    taper_leading_axis,
    taper_trailing_axis,
    depth_layer_factors,
    measured_correlations,
    visibility_groups_table,
    antenna_links,
    complex_receiver_factors,
):
    sizes = tuple(lax.axis_size(name) for name in ("facet", "pol", "tm"))
    subgrids, pols, owners = sizes
    slots = taper_leading_axis.shape[2]
    quarter = measured_correlations.shape[3]
    rows = tile_spectral_lines.shape[3]

    block_table = visibility_groups_table.reshape(3, visibility_groups_table.shape[3])
    observed = measured_correlations.reshape(2 * NPOL, quarter)

    contrib, gains, idents = fourier(
        tile_spectral_lines[:, 0],
        subgrids,
        slots,
        block_table,
        antenna_links,
        complex_receiver_factors,
    )
    table_re, table_im, second = [jnp.asarray(t) for t in subgrid_tables()]
    cosine, sine = chirp_line()
    own_count = NST // (subgrids * pols * owners)
    residual, grad = predict(
        sizes,
        own_count,
        contrib,
        taper_leading_axis.reshape(slots, SG),
        taper_trailing_axis.reshape(slots, SG),
        depth_layer_factors.reshape(NW, slots),
        observed,
        gains,
        idents,
        table_re.reshape(FGRID, owners, rows, SG),
        table_im.reshape(FGRID, owners, rows, SG),
        second,
        jnp.asarray(np.stack([cosine, sine])),
    )
    gain_grad = jnp.transpose(grad, (1, 2, 0)).reshape(own_count, 4 * NCH)
    return residual.reshape(1, 2 * NPOL, 1, quarter), gain_grad


def solution(mesh):
    return jax.shard_map(
        on_device,
        mesh=mesh,
        in_specs=(
            P("facet", "pol", None, "tm", None),
            P("facet", "tm", None, None),
            P("facet", "tm", None, None),
            P("facet", "tm", None, None),
            P("facet", None, "tm", "pol"),
            P("facet", "tm", None, None),
            P(),
            P(),
        ),
        out_specs=(P("facet", None, "tm", "pol"), P(("facet", "pol", "tm"), None)),
        check_vma=False,
    )
```

profile of v0, /device:TPU:0, one launch (start us, length us, event | category | flops | bytes accessed | tf_op | source)
XLA Modules:
  0.0 39.3 jit_solution(6268425656945700689)
XLA Ops:
  0.6 0.0 copy-start.1
  0.6 0.0 copy-start.2
  0.7 0.0 copy-start.6
  0.7 0.0 copy-start
  0.7 0.0 copy-start.5
  0.7 0.0 copy-start.7
  0.7 0.0 copy-start.4
  0.7 0.0 copy-start.3
  0.7 0.8 %copy.24 = s32[1,1,3,8]{3,2,1,0:T(4,128)S(1)} copy(s32[1,1,3,8]{3,1,2,0:T(1,128)} %param.21) | data formatting | bytes 192
  1.6 9.0 %shard_map.167 = (bf16[4,2,32,1024]{3,2,1,0:T(8,128)(2,1)S(1)}, f32[8,128]{1,0:T(8,128)S(1)}, f32[8,128]{1,0:T(8,128)S(1)}) custom-call(s32[3,8]{1,0:T(4,128)S(1)} %bitcast.16, s32[2,130816]{1,0:T(2,128)} %links_ref.1, f32[256,4,512]{2,1,0:T(4,128)} %gain_ref.1, f32[64,512]{1,0:T(8,128)} %constant.16.clone.p_ref, f32[64,512]{1,0:T(8,128)} %constant.17.clone.q_ref, ...), custom_call_target="tpu_custom_call" | custom-call | tf_op jit(solution)/shard_map/pallas_call | solution.py:199
  10.6 0.0 copy-done.1
  10.6 0.0 copy-done.2
  10.6 0.0 copy-done.6
  10.6 0.0 copy-done
  10.6 0.0 copy-done.5
  10.6 0.0 copy-done.7
  10.7 0.0 copy-done.4
  10.7 0.0 copy-done.3
  10.7 27.0 %shard_map.168 = (f32[8,32]{1,0:T(8,128)S(1)}, f32[4,16,256]{2,1,0:T(8,128)S(1)}) custom-call(bf16[4,2,32,1024]{3,2,1,0:T(8,128)(2,1)S(1)} %get-tuple-element.7.contrib_ref, bf16[128,512]{1,0:T(8,128)(2,1)S(1)} %bitcast.13, bf16[128,512]{1,0:T(8,128)(2,1)S(1)} %bitcast.14, bf16[2,128]{1,0:T(2,128)(2,1)S(1)} %bitcast.19, f32[8,32]{1,0:T(8,128)S(1)} %bitcast.17, ...), custom_call_target="tpu_custom_call" | custom-call | tf_op jit(solution)/shard_map/pallas_call | solution.py:566
  37.7 0.2 copy.19
  37.9 0.8 %copy.21 = f32[16,1024]{1,0:T(8,128)} copy(f32[16,1024]{0,1:T(8,128)S(1)} %bitcast.21) | data formatting | bytes 131072
  38.8 0.6 %copy.26 = f32[1,8,1,32]{3,2,1,0:T(1,128)} copy(f32[1,8,1,32]{3,2,1,0:T(1,128)S(1)} %bitcast.18) | data formatting | bytes 2048
Async XLA Ops:
  0.6 10.0 %copy-start.1 = (bf16[8,2,32,512]{3,2,1,0:T(8,128)(2,1)S(1)}, bf16[8,2,32,512]{3,2,1,0:T(8,128)(2,1)}, u32[]{:S(2)}) copy-start(bf16[8,2,32,512]{3,2,1,0:T(8,128)(2,1)} %constant.31.table_im_ref) | copy-start | bytes 1572868
  0.6 10.0 %copy-start.2 = (bf16[8,2,32,512]{3,2,1,0:T(8,128)(2,1)S(1)}, bf16[8,2,32,512]{3,2,1,0:T(8,128)(2,1)}, u32[]{:S(2)}) copy-start(bf16[8,2,32,512]{3,2,1,0:T(8,128)(2,1)} %constant.30.table_re_ref) | copy-start | bytes 1572868
  0.7 10.0 %copy-start.6 = (f32[2,512]{1,0:T(2,128)S(1)}, f32[2,512]{1,0:T(2,128)}, u32[]{:S(2)}) copy-start(f32[2,512]{1,0:T(2,128)} %constant.23.clone.chirp_ref) | copy-start | bytes 12292
  0.7 10.0 %copy-start = (bf16[512,1024]{1,0:T(8,128)(2,1)S(1)}, bf16[512,1024]{1,0:T(8,128)(2,1)}, u32[]{:S(2)}) copy-start(bf16[512,1024]{1,0:T(8,128)(2,1)} %constant.22.clone.second_ref) | copy-start | bytes 3145732
  0.7 10.0 %copy-start.5 = (f32[1,8,1,32]{3,2,1,0:T(1,128)S(1)}, f32[1,8,1,32]{3,2,1,0:T(1,128)}, u32[]{:S(2)}) copy-start(f32[1,8,1,32]{3,2,1,0:T(1,128)} %param.20) | copy-start | bytes 3076
  0.7 10.0 %copy-start.7 = (bf16[1,1,2,128]{3,2,1,0:T(2,128)(2,1)S(1)}, bf16[1,1,2,128]{3,2,1,0:T(2,128)(2,1)}, u32[]{:S(2)}) copy-start(bf16[1,1,2,128]{3,2,1,0:T(2,128)(2,1)} %param.19) | copy-start | bytes 1540
  0.7 10.0 %copy-start.4 = (bf16[1,1,128,512]{3,2,1,0:T(8,128)(2,1)S(1)}, bf16[1,1,128,512]{3,2,1,0:T(8,128)(2,1)}, u32[]{:S(2)}) copy-start(bf16[1,1,128,512]{3,2,1,0:T(8,128)(2,1)} %param.18) | copy-start | bytes 393220
  0.7 10.0 %copy-start.3 = (bf16[1,1,128,512]{3,2,1,0:T(8,128)(2,1)S(1)}, bf16[1,1,128,512]{3,2,1,0:T(8,128)(2,1)}, u32[]{:S(2)}) copy-start(bf16[1,1,128,512]{3,2,1,0:T(8,128)(2,1)} %param.17) | copy-start | bytes 393220
where the time goes:
time: 39.5 us; the launch traced here: 39.3 us
  Pallas kernels  36.1 us (91%)
  local copies, waits for them, and re-layouts  2.5 us (6%)
  between operations  0.78 us (2%)
    pallas_call x1, Pallas kernels, predict(): pl.pallas_call(functools.partial(predict_kernel, sizes), out_shape=(jax.S...  27 us
    pallas_call x1, Pallas kernels, fourier(): pl.pallas_call(fourier_kernel, out_shape=(jax.ShapeDtypeStruct(out, jnp.b...  9.04 us
    unnamed x19, local copies, waits for them, and re-layouts  2.27 us

commit v1 on v0

--- a/solution.py
+++ b/solution.py
@@ -18,6 +18,7 @@
 NCH = 256
 NST = 512
 CHUNK = 1024
+PIECES = 2
 
 w_chirp = 0.37
 grad_scale = 0.1
@@ -600,6 +601,542 @@
     )(*operands)
 
 
+def gather_lookups(block_ref, links_ref, gain_ref, gains_ref, idents_ref):
+    blocks = block_ref.shape[2]
+    slots = idents_ref.shape[1]
+    span = slots + 128
+    lane = lax.broadcasted_iota(jnp.int32, (1, slots), 1)
+    place = lax.broadcasted_iota(jnp.int32, (span, slots), 0)
+    lane_tall = lax.broadcasted_iota(jnp.int32, (span, slots), 1)
+    begin = jnp.int32(0)
+    member, picks, windows, tables = [], [], [], []
+    channel = jnp.zeros((1, slots), jnp.float32)
+    alive = jnp.zeros((1, slots), jnp.float32)
+    for b in range(blocks):
+        chosen, offset, amount = [block_ref[k, 0, b] for k in range(3)]
+        row = jnp.minimum(lax.div(offset, 128), links_ref.shape[0] - span // 128)
+        first = row * 128
+        windows += [links_ref[row + k] for k in range(span // 128)]
+        tables.append(gain_ref[chosen])
+        inside = jnp.where((lane >= begin) & (lane < begin + amount), 1.0, 0.0)
+        member.append(inside)
+        alive += inside
+        channel += inside * chosen.astype(jnp.float32)
+        hit = place == lane_tall + (offset - first - begin)
+        picks.append((jnp.where(hit, 1.0, 0.0) * inside).astype(jnp.bfloat16))
+        begin = begin + amount
+    links = jnp.concatenate(windows, axis=1)
+    upper = links // 16
+    lower = links - 16 * upper
+    pieces = jnp.concatenate([upper, lower], axis=0).astype(jnp.float32).astype(jnp.bfloat16)
+    found = jnp.dot(
+        pieces, jnp.concatenate(picks, axis=0), preferred_element_type=jnp.float32
+    )
+    stations = 16.0 * found[0:2] + found[2:4]
+    table = jnp.concatenate(tables, axis=0)
+    high = table.astype(jnp.bfloat16)
+    rest = table - high.astype(jnp.float32)
+    middle = rest.astype(jnp.bfloat16)
+    low = (rest - middle.astype(jnp.float32)).astype(jnp.bfloat16)
+    split = jnp.concatenate([high, middle, low], axis=0)
+    size = table.shape[0]
+    names = lax.broadcasted_iota(jnp.int32, (table.shape[1], 1), 0).astype(jnp.float32)
+    for side in range(2):
+        pick = jnp.where(names == stations[side : side + 1], 1.0, 0.0).astype(jnp.bfloat16)
+        three = jnp.dot(split, pick, preferred_element_type=jnp.float32)
+        rows = three[:size] + three[size : 2 * size] + three[2 * size :]
+        chosen = member[0] * rows[0:4]
+        for b in range(1, blocks):
+            chosen = chosen + member[b] * rows[4 * b : 4 * b + 4]
+        gains_ref[4 * side : 4 * side + 4, :] = chosen
+    idents_ref[0:2, :] = stations
+    idents_ref[2:3, :] = channel
+    idents_ref[3:4, :] = alive
+    idents_ref[4:8, :] = jnp.zeros((4, slots), jnp.float32)
+
+
+def fused_kernel(
+    sizes,
+    block_hbm,
+    links_hbm,
+    gain_hbm,
+    p_hbm,
+    q_hbm,
+    c_hbm,
+    s_hbm,
+    x_hbm,
+    lead_hbm,
+    trail_hbm,
+    depth_hbm,
+    observed_hbm,
+    table_re_hbm,
+    table_im_hbm,
+    second_hbm,
+    chirp_hbm,
+    residual_ref,
+    grad_ref,
+    block_ref,
+    links_ref,
+    gain_ref,
+    p_ref,
+    q_ref,
+    c_ref,
+    s_ref,
+    x_ref,
+    lead_ref,
+    trail_ref,
+    depth_ref,
+    observed_ref,
+    table_ref,
+    second_ref,
+    chirp_ref,
+    factors,
+    contrib,
+    got,
+    tapers,
+    right,
+    left,
+    gains_ref,
+    idents,
+    part_out,
+    part_in,
+    observed_out,
+    observed_in,
+    record_out,
+    record_in,
+    load_sem,
+    chunk_sem,
+    got_send,
+    got_recv,
+    taper_send,
+    taper_recv,
+    observed_send,
+    observed_recv,
+    part_send,
+    part_recv,
+    ident_send,
+    ident_recv,
+    record_send,
+    record_recv,
+):
+    subgrids, pols, owners = sizes
+    z, p, t = lax.axis_index("facet"), lax.axis_index("pol"), lax.axis_index("tm")
+    slots = lead_ref.shape[0]
+    facets, _, rows, length = x_ref.shape
+    _, groups, _, width = contrib.shape
+    mesh_id = pl.DeviceIdType.MESH
+
+    def remote(src, dst, send, recv, peer):
+        return pltpu.make_async_remote_copy(
+            src_ref=src,
+            dst_ref=dst,
+            send_sem=send,
+            recv_sem=recv,
+            device_id=peer,
+            device_id_type=mesh_id,
+        )
+
+    across_total = subgrids * owners
+    plane_total = pols * owners
+    across = z * owners + t
+    plane = p * owners + t
+
+    def across_peer(d):
+        other = lax.rem(across + d, across_total)
+        return other, (other // owners, p, lax.rem(other, owners))
+
+    def plane_peer(d):
+        other = lax.rem(plane + d, plane_total)
+        return other, (z, other // owners, lax.rem(other, owners))
+
+    barrier = pltpu.get_barrier_semaphore()
+    for d in range(1, across_total):
+        pl.semaphore_signal(barrier, inc=1, device_id=across_peer(d)[1], device_id_type=mesh_id)
+    for d in range(1, pols):
+        q = lax.rem(p + d, pols)
+        for o in range(owners):
+            pl.semaphore_signal(barrier, inc=1, device_id=(z, q, o), device_id_type=mesh_id)
+
+    per_chunk = FGRID // PIECES
+    chunks = facets // per_chunk
+    x_loads = [
+        pltpu.make_async_copy(
+            x_hbm.at[pl.ds(c * per_chunk, per_chunk)],
+            x_ref.at[pl.ds(c * per_chunk, per_chunk)],
+            chunk_sem.at[c],
+        )
+        for c in range(chunks)
+    ]
+    pairs = [
+        (c_hbm, c_ref),
+        (s_hbm, s_ref),
+        (p_hbm, p_ref),
+        (q_hbm, q_ref),
+        (lead_hbm, lead_ref),
+        (trail_hbm, trail_ref),
+        (depth_hbm, depth_ref),
+        (observed_hbm, observed_ref),
+        (chirp_hbm, chirp_ref),
+        (second_hbm, second_ref),
+        (table_re_hbm.at[:, t], table_ref.at[0]),
+        (table_im_hbm.at[:, t], table_ref.at[1]),
+        (block_hbm, block_ref),
+        (links_hbm, links_ref),
+        (gain_hbm, gain_ref),
+    ]
+    loads = [
+        pltpu.make_async_copy(src, dst, load_sem.at[k]) for k, (src, dst) in enumerate(pairs)
+    ]
+    for copy in loads[:4]:
+        copy.start()
+    x_loads[0].start()
+    for copy in loads[4:9]:
+        copy.start()
+    for copy in x_loads[1:]:
+        copy.start()
+    for copy in loads[9:]:
+        copy.start()
+
+    for copy in loads[:4]:
+        copy.wait()
+    spread = c_ref.shape[0]
+    cosine, sine = c_ref[...], s_ref[...]
+    for part in range(length // spread):
+        factors[part * spread : (part + 1) * spread, :] = (
+            p_ref[part : part + 1, :] * cosine + q_ref[part : part + 1, :] * sine
+        ).astype(jnp.bfloat16)
+
+    lane = lax.broadcasted_iota(jnp.int32, (rows, 2 * MC), 1)
+    sign = jnp.where(lane < MC, -1.0, 1.0)
+    part_width = width // PIECES
+    partner = lax.rem(t + 1, owners)
+    copies, taper_copies, observed_copies = [], [], []
+    for c in range(chunks):
+        x_loads[c].wait()
+        x = x_ref[c * per_chunk : (c + 1) * per_chunk].reshape(per_chunk * 2 * rows, length)
+        total = jnp.dot(x, factors[...], preferred_element_type=jnp.float32)
+        group, piece = c // PIECES, c % PIECES
+        for s in range(subgrids):
+            cut = slice(s * 2 * MC, (s + 1) * 2 * MC)
+            for f in range(per_chunk):
+                first = total[2 * f * rows : (2 * f + 1) * rows, cut]
+                second = total[(2 * f + 1) * rows : (2 * f + 2) * rows, cut]
+                j = piece * per_chunk + f
+                contrib[s, group, :, j * 2 * MC : (j + 1) * 2 * MC] = (
+                    first + sign * pltpu.roll(second, MC, 1)
+                ).astype(jnp.bfloat16)
+        if c == 0:
+            pl.semaphore_wait(barrier, across_total - 1 + (pols - 1) * owners)
+        lanes = pl.ds(piece * part_width, part_width)
+        for d in sorted(range(1, subgrids), key=lambda d: -min(d, subgrids - d)):
+            other = lax.rem(z + d, subgrids)
+            copy = remote(
+                contrib.at[other, group, :, lanes],
+                got.at[z, group, :, lanes],
+                got_send.at[c * subgrids + d],
+                got_recv.at[c * subgrids + d],
+                (other, p, t),
+            )
+            copy.start()
+            copies.append(copy)
+        if c == 0:
+            for copy in loads[4:9]:
+                copy.wait()
+            taper_copies = [
+                remote(ref, tapers.at[k], taper_send.at[k], taper_recv.at[k], (z, p, partner))
+                for k, ref in enumerate((trail_ref, lead_ref))
+            ]
+            quarter = observed_ref.shape[1]
+            place = lax.broadcasted_iota(jnp.int32, (2 * NPOL, slots), 1)
+            observed_out[...] = jnp.where(
+                (place >= p * quarter) & (place < (p + 1) * quarter),
+                jnp.concatenate([observed_ref[...]] * pols, axis=1),
+                0.0,
+            )
+            for d in range(1, pols):
+                q = lax.rem(p + d, pols)
+                observed_copies.append(
+                    remote(
+                        observed_out,
+                        observed_in.at[p],
+                        observed_send.at[d],
+                        observed_recv.at[d],
+                        (z, q, t),
+                    )
+                )
+            for copy in taper_copies + observed_copies:
+                copy.start()
+
+    got[z] = contrib[z]
+    for copy in loads[9:]:
+        copy.wait()
+    gather_lookups(block_ref, links_ref, gain_ref, gains_ref, idents.at[across])
+    ident_copies = []
+    for d in range(1, across_total):
+        other, peer = across_peer(d)
+        ident_copies.append(
+            remote(idents.at[across], idents.at[across], ident_send.at[d], ident_recv.at[d], peer)
+        )
+    for copy in ident_copies:
+        copy.start()
+
+    table_re = jnp.concatenate([table_ref[0, i] for i in range(FGRID)], axis=0)
+    table_im = jnp.concatenate([table_ref[1, i] for i in range(FGRID)], axis=0)
+    turn = jnp.where(
+        lax.broadcasted_iota(jnp.int32, (3 * slots, 2 * MC), 1) < MC, -1.0, 1.0
+    )
+
+    def prepare(owner, trail, lead):
+        trail3 = chirped_rows(trail, chirp_ref)
+        a = jnp.dot(trail3, second_ref[...], preferred_element_type=jnp.float32)
+        b = jnp.concatenate(
+            [
+                turn * pltpu.roll(a[:, j * 2 * MC : (j + 1) * 2 * MC], MC, 1)
+                for j in range(a.shape[1] // (2 * MC))
+            ],
+            axis=1,
+        )
+        n0, n1, n2 = slice(0, slots), slice(slots, 2 * slots), slice(2 * slots, 3 * slots)
+        right[owner, 0:slots, :] = a[n0].astype(jnp.bfloat16)
+        right[owner, slots : 2 * slots, :] = (a[n1] - b[n2]).astype(jnp.bfloat16)
+        right[owner, 2 * slots : 3 * slots, :] = b[n0].astype(jnp.bfloat16)
+        right[owner, 3 * slots : 4 * slots, :] = (b[n1] + a[n2]).astype(jnp.bfloat16)
+        lead3 = chirped_rows(lead, chirp_ref)
+        u = nt_dot(table_re, lead3)
+        v = nt_dot(table_im, lead3)
+        left[owner, 0] = u[:, n0]
+        left[owner, 1] = v[:, n0]
+        left[owner, 2] = u[:, n1] - v[:, n2]
+        left[owner, 3] = u[:, n2] + v[:, n1]
+
+    prepare(t, trail_ref[...], lead_ref[...])
+    for copy in taper_copies:
+        copy.wait()
+    prepare(partner, tapers[0], tapers[1])
+    for copy in copies:
+        copy.wait()
+    whole = got[...].reshape(subgrids * groups * rows, width)
+    for o in range(owners):
+        across_v = nt_dot(whole, right[o])
+        for w in range(NW):
+            g_re = across_v[:, w * slots : (w + 1) * slots]
+            g_im = across_v[:, (NW + w) * slots : (NW + w + 1) * slots]
+            l_re, l_im = left[o, 2 * w], left[o, 2 * w + 1]
+            part_out[o, 2 * w : 2 * w + 1, :] = jnp.sum(l_re * g_re - l_im * g_im, axis=0, keepdims=True)
+            part_out[o, 2 * w + 1 : 2 * w + 2, :] = jnp.sum(
+                l_re * g_im + l_im * g_re, axis=0, keepdims=True
+            )
+        part_out[o, 2 * NW :, :] = jnp.zeros((8 - 2 * NW, slots), jnp.float32)
+
+    part_copies = []
+    for d in range(1, plane_total):
+        other, peer = plane_peer(d)
+        part_copies.append(
+            remote(
+                part_out.at[lax.rem(other, owners)],
+                part_in.at[plane],
+                part_send.at[d],
+                part_recv.at[d],
+                peer,
+            )
+        )
+    for copy in part_copies:
+        copy.start()
+    part_in[plane] = part_out[t]
+    observed_in[p] = observed_out[...]
+    for copy in observed_copies:
+        copy.wait()
+    observed = observed_in[0]
+    for q in range(1, pols):
+        observed = observed + observed_in[q]
+    depth = depth_ref[...].astype(jnp.float32)
+    own_idents = idents[across]
+    gains = gains_ref[...]
+    for copy in ident_copies:
+        copy.wait()
+    names = jnp.concatenate([idents[d, 0:3] for d in range(across_total)], axis=1)
+    own_count = grad_ref.shape[0]
+    index = (z * pols + p) * owners + t
+    mine = (index * own_count + lax.broadcasted_iota(jnp.int32, (own_count, 1), 0)).astype(
+        jnp.float32
+    )
+    first_here = jnp.where(mine == names[0:1], 1.0, 0.0)
+    second_here = jnp.where(mine == names[1:2], 1.0, 0.0)
+    channel_ids = lax.broadcasted_iota(jnp.int32, (NCH, 1), 0).astype(jnp.float32)
+    onehot = jnp.where(channel_ids == names[2:3], 1.0, 0.0).astype(jnp.bfloat16)
+    for copy in part_copies:
+        copy.wait()
+
+    pred = []
+    per_pol = part_in.shape[0] // NPOL
+    for q in range(NPOL):
+        block = part_in[q * per_pol]
+        for o in range(1, per_pol):
+            block = block + part_in[q * per_pol + o]
+        pred.append(
+            tuple(
+                sum(depth[w : w + 1] * block[2 * w + c : 2 * w + c + 1] for w in range(NW))
+                for c in range(2)
+            )
+        )
+    residual, leading, trailing = model_terms(
+        pred,
+        [observed[k : k + 1] for k in range(2 * NPOL)],
+        [gains[k : k + 1] for k in range(4)],
+        [gains[4 + k : 5 + k] for k in range(4)],
+        own_idents[3:4],
+    )
+    record_out[...] = jnp.concatenate(leading + trailing, axis=0)
+    record_copies = []
+    for d in range(1, across_total):
+        other, peer = across_peer(d)
+        record_copies.append(
+            remote(record_out, record_in.at[across], record_send.at[d], record_recv.at[d], peer)
+        )
+    for copy in record_copies:
+        copy.start()
+    record_in[across] = record_out[...]
+    rest = jnp.concatenate(residual, axis=0)
+    quarter = observed_ref.shape[1]
+    own_rest = jnp.zeros((2 * NPOL, quarter), jnp.float32)
+    for q in range(pols):
+        own_rest = jnp.where(p == q, rest[:, q * quarter : (q + 1) * quarter], own_rest)
+    residual_ref[...] = own_rest
+    for copy in record_copies:
+        copy.wait()
+
+    piece = jnp.concatenate([record_in[d] for d in range(across_total)], axis=1)
+    weighted = jnp.concatenate(
+        [
+            first_here * piece[k : k + 1] + second_here * piece[4 + k : 5 + k]
+            for k in range(4)
+        ],
+        axis=0,
+    )
+    high = weighted.astype(jnp.bfloat16)
+    low = (weighted - high.astype(jnp.float32)).astype(jnp.bfloat16)
+    summed = nt_dot(high, onehot) + nt_dot(low, onehot)
+    lane_group = lax.broadcasted_iota(jnp.int32, (own_count, 128), 1) // 32
+    mixed = []
+    for g in range(NCH // 32):
+        base = g // 4 * 128
+        built = None
+        for k in range(4):
+            block = summed[k * own_count : (k + 1) * own_count, base : base + 128]
+            shift = 32 * (k - g % 4) % 128
+            block = pltpu.roll(block, shift, 1) if shift else block
+            built = block if built is None else jnp.where(lane_group == k, block, built)
+        mixed.append(grad_scale * built)
+    mixed = jnp.concatenate(mixed, axis=0)
+    high = mixed.astype(jnp.bfloat16)
+    low = (mixed - high.astype(jnp.float32)).astype(jnp.bfloat16)
+    came = lax.broadcasted_iota(jnp.int32, (128, 128), 0)
+    goes = lax.broadcasted_iota(jnp.int32, (128, 128), 1)
+    order = jnp.where(goes == came % 32 * 4 + came // 32, 1.0, 0.0).astype(jnp.bfloat16)
+    placed = jnp.dot(
+        jnp.concatenate([high, low], axis=0), order, preferred_element_type=jnp.float32
+    )
+    placed = placed[: mixed.shape[0]] + placed[mixed.shape[0] :]
+    for g in range(NCH // 32):
+        grad_ref[:, g * 128 : (g + 1) * 128] = placed[g * own_count : (g + 1) * own_count]
+
+
+def emit_kernel(residual_ref, grad_ref, residual_out, grad_out, sems):
+    copies = [
+        pltpu.make_async_copy(residual_ref, residual_out, sems.at[0]),
+        pltpu.make_async_copy(grad_ref, grad_out, sems.at[1]),
+    ]
+    for copy in copies:
+        copy.start()
+    for copy in copies:
+        copy.wait()
+
+
+def fused(sizes, own_count, *operands):
+    subgrids, pols, owners = sizes
+    block_table, links, gains = operands[0:3]
+    x, lead, trail, depth, observed = operands[7:12]
+    facets, _, rows, length = x.shape
+    slots = lead.shape[0]
+    width = subgrids * 2 * MC
+    spread = FS // MC
+    groups = facets // FGRID
+    chunks = facets // (FGRID // PIECES)
+    hbm = pl.BlockSpec(memory_space=pltpu.HBM)
+    vmem = pl.BlockSpec(memory_space=pltpu.VMEM)
+    dma = lambda n: pltpu.SemaphoreType.DMA((n,))
+    held = lambda a: pltpu.VMEM(a.shape, a.dtype)
+    across_total, plane_total = subgrids * owners, pols * owners
+    f32, bf16 = jnp.float32, jnp.bfloat16
+    residual, grad = pl.pallas_call(
+        functools.partial(fused_kernel, sizes),
+        out_shape=(
+            jax.ShapeDtypeStruct(observed.shape, f32),
+            jax.ShapeDtypeStruct((own_count, 4 * NCH), f32),
+        ),
+        in_specs=[hbm] * len(operands),
+        out_specs=(vmem, vmem),
+        scratch_shapes=[
+            pltpu.SMEM(block_table.shape, jnp.int32),
+            held(links),
+            held(gains),
+            pltpu.VMEM((length // spread, width), f32),
+            pltpu.VMEM((length // spread, width), f32),
+            pltpu.VMEM((spread, width), f32),
+            pltpu.VMEM((spread, width), f32),
+            held(x),
+            held(lead),
+            held(trail),
+            held(depth),
+            held(observed),
+            pltpu.VMEM((2, FGRID, rows, SG), bf16),
+            pltpu.VMEM((SG, 2 * SG), bf16),
+            pltpu.VMEM((2, SG), f32),
+            pltpu.VMEM((length, width), bf16),
+            pltpu.VMEM((subgrids, groups, rows, 2 * SG), bf16),
+            pltpu.VMEM((subgrids, groups, rows, 2 * SG), bf16),
+            pltpu.VMEM((2, slots, SG), bf16),
+            pltpu.VMEM((owners, 2 * NW * slots, 2 * SG), bf16),
+            pltpu.VMEM((owners, 4, FGRID * rows, slots), f32),
+            pltpu.VMEM((8, slots), f32),
+            pltpu.VMEM((across_total, 8, slots), f32),
+            pltpu.VMEM((owners, 8, slots), f32),
+            pltpu.VMEM((plane_total, 8, slots), f32),
+            pltpu.VMEM((8, slots), f32),
+            pltpu.VMEM((pols, 8, slots), f32),
+            pltpu.VMEM((8, slots), f32),
+            pltpu.VMEM((across_total, 8, slots), f32),
+            dma(15),
+            dma(chunks),
+            dma(chunks * subgrids),
+            dma(chunks * subgrids),
+            dma(2),
+            dma(2),
+            dma(pols),
+            dma(pols),
+            dma(plane_total),
+            dma(plane_total),
+            dma(across_total),
+            dma(across_total),
+            dma(across_total),
+            dma(across_total),
+        ],
+        compiler_params=pltpu.CompilerParams(
+            collective_id=0, has_side_effects=True, vmem_limit_bytes=56 << 20
+        ),
+    )(*[pltpu.with_memory_space_constraint(a, pltpu.HBM) for a in operands])
+    return pl.pallas_call(
+        emit_kernel,
+        out_shape=(
+            jax.ShapeDtypeStruct(residual.shape, f32),
+            jax.ShapeDtypeStruct(grad.shape, f32),
+        ),
+        in_specs=[vmem] * 2,
+        out_specs=[hbm] * 2,
+        scratch_shapes=[dma(2)],
+    )(residual, grad)
+
+
 def on_device(
     tile_spectral_lines,
     taper_leading_axis,
@@ -618,6 +1155,28 @@
 
     block_table = visibility_groups_table.reshape(3, visibility_groups_table.shape[3])
     observed = measured_correlations.reshape(2 * NPOL, quarter)
+
+    if tile_spectral_lines.shape[0] % FGRID == 0:
+        table_re, table_im, second = [jnp.asarray(t) for t in subgrid_tables()]
+        own_count = NST // (subgrids * pols * owners)
+        residual, gain_grad = fused(
+            sizes,
+            own_count,
+            visibility_groups_table.reshape(3, 1, visibility_groups_table.shape[3]),
+            jnp.transpose(antenna_links.reshape(2, -1, 128), (1, 0, 2)),
+            complex_receiver_factors,
+            *[jnp.asarray(t) for t in fourier_factors(subgrids)],
+            tile_spectral_lines[:, 0],
+            taper_leading_axis.reshape(slots, SG),
+            taper_trailing_axis.reshape(slots, SG),
+            depth_layer_factors.reshape(NW, slots),
+            observed,
+            table_re.reshape(FGRID, owners, rows, SG),
+            table_im.reshape(FGRID, owners, rows, SG),
+            second,
+            jnp.asarray(np.stack(chirp_line())),
+        )
+        return residual.reshape(1, 2 * NPOL, 1, quarter), gain_grad
 
     contrib, gains, idents = fourier(
         tile_spectral_lines[:, 0],

time: 39.5 us -> 32.4 us (0.82)
  Pallas kernels: 36.1 us -> 31.6 us
  local copies, waits for them, and re-layouts: 2.5 us -> 0 us
    pallas_call x2, Pallas kernels: 36.1 us -> 31.6 us  [the longest x1 30.1 us: fused(): pl.pallas_call(functools.partial(fused_kernel, sizes), out_shape=(jax.Sha...]
    unnamed x19 -> x0, local copies, waits for them, and re-layouts: 2.27 us -> none
where the time goes in v1:
time: 32.4 us; the launch traced here: 32.3 us
  Pallas kernels  31.6 us (98%)
  between operations  0.64 us (2%)
    pallas_call x1, Pallas kernels, fused(): pl.pallas_call(functools.partial(fused_kernel, sizes), out_shape=(jax.Sha...  30.1 us
    pallas_call x1, Pallas kernels, fused(): pl.pallas_call(emit_kernel, out_shape=(jax.ShapeDtypeStruct(residual.shap...  1.49 us

profile of v1, /device:TPU:0, one launch (start us, length us, event | category | flops | bytes accessed | tf_op | source)
XLA Modules:
  0.0 32.3 jit_solution(4863795155876435299)
XLA Ops:
  0.6 30.1 %shard_map.167 = (f32[8,32]{1,0:T(8,128)}, f32[16,1024]{1,0:T(8,128)}) custom-call(s32[3,1,8]{2,1,0:T(1,128)} %bitcast.17, s32[1022,2,128]{2,1,0:T(2,128)} %bitcast.13, f32[256,4,512]{2,1,0:T(4,128)} %gain_hbm.1, f32[64,512]{1,0:T(8,128)} %constant.19.clone.p_hbm, f32[64,512]{1,0:T(8,128)} %constant.20.clone.q_hbm, f32[64,512]{1,0:T(8,128)} %constant.21.clone.c_hbm, ...), custom_call_target="tpu_custom_call" | custom-call | tf_op jit(solution)/shard_map/pallas_call | solution.py:1071
  30.8 1.5 %shard_map.168 = (f32[8,32]{1,0:T(8,128)}, f32[16,1024]{1,0:T(8,128)}) custom-call(f32[8,32]{1,0:T(8,128)} %get-tuple-element.6.residual_ref, f32[16,1024]{1,0:T(8,128)} %get-tuple-element.7.grad_ref), custom_call_target="tpu_custom_call" | custom-call | tf_op jit(solution)/shard_map/pallas_call | solution.py:1128

commit v2 on v1

--- a/solution.py
+++ b/solution.py
@@ -697,13 +697,14 @@
     right,
     left,
     gains_ref,
-    idents,
+    idents_ref,
+    depths,
+    side,
     part_out,
     part_in,
     observed_out,
     observed_in,
-    record_out,
-    record_in,
+    rests,
     load_sem,
     chunk_sem,
     got_send,
@@ -712,12 +713,10 @@
     taper_recv,
     observed_send,
     observed_recv,
+    side_send,
+    side_recv,
     part_send,
     part_recv,
-    ident_send,
-    ident_recv,
-    record_send,
-    record_recv,
 ):
     subgrids, pols, owners = sizes
     z, p, t = lax.axis_index("facet"), lax.axis_index("pol"), lax.axis_index("tm")
@@ -737,17 +736,11 @@
         )
 
     across_total = subgrids * owners
-    plane_total = pols * owners
     across = z * owners + t
-    plane = p * owners + t
 
     def across_peer(d):
         other = lax.rem(across + d, across_total)
         return other, (other // owners, p, lax.rem(other, owners))
-
-    def plane_peer(d):
-        other = lax.rem(plane + d, plane_total)
-        return other, (z, other // owners, lax.rem(other, owners))
 
     barrier = pltpu.get_barrier_semaphore()
     for d in range(1, across_total):
@@ -757,6 +750,13 @@
         for o in range(owners):
             pl.semaphore_signal(barrier, inc=1, device_id=(z, q, o), device_id_type=mesh_id)
 
+    offsets = [
+        (dz, dp, dt)
+        for dz in sorted(range(subgrids), key=lambda d: -min(d, subgrids - d))
+        for dp in reversed(range(pols))
+        for dt in range(owners)
+    ]
+    offsets.remove((0, 0, 0))
     per_chunk = FGRID // PIECES
     chunks = facets // per_chunk
     x_loads = [
@@ -843,8 +843,14 @@
             for copy in loads[4:9]:
                 copy.wait()
             taper_copies = [
-                remote(ref, tapers.at[k], taper_send.at[k], taper_recv.at[k], (z, p, partner))
-                for k, ref in enumerate((trail_ref, lead_ref))
+                remote(src, dst, taper_send.at[k], taper_recv.at[k], (z, p, partner))
+                for k, (src, dst) in enumerate(
+                    [
+                        (trail_ref, tapers.at[0]),
+                        (lead_ref, tapers.at[1]),
+                        (depth_ref, depths),
+                    ]
+                )
             ]
             quarter = observed_ref.shape[1]
             place = lax.broadcasted_iota(jnp.int32, (2 * NPOL, slots), 1)
@@ -870,14 +876,23 @@
     got[z] = contrib[z]
     for copy in loads[9:]:
         copy.wait()
-    gather_lookups(block_ref, links_ref, gain_ref, gains_ref, idents.at[across])
-    ident_copies = []
+    gather_lookups(block_ref, links_ref, gain_ref, gains_ref, idents_ref)
+    observed_in[p] = observed_out[...]
+    for copy in observed_copies:
+        copy.wait()
+    observed = observed_in[0]
+    for q in range(1, pols):
+        observed = observed + observed_in[q]
+    side[across, 0:8] = gains_ref[...]
+    side[across, 8:16] = observed
+    side[across, 16:20] = idents_ref[0:4]
+    side_copies = []
     for d in range(1, across_total):
         other, peer = across_peer(d)
-        ident_copies.append(
-            remote(idents.at[across], idents.at[across], ident_send.at[d], ident_recv.at[d], peer)
-        )
-    for copy in ident_copies:
+        side_copies.append(
+            remote(side.at[across], side.at[across], side_send.at[d], side_recv.at[d], peer)
+        )
+    for copy in side_copies:
         copy.start()
 
     table_re = jnp.concatenate([table_ref[0, i] for i in range(FGRID)], axis=0)
@@ -918,97 +933,89 @@
     whole = got[...].reshape(subgrids * groups * rows, width)
     for o in range(owners):
         across_v = nt_dot(whole, right[o])
+        sums = [0.0, 0.0]
+        weights = jnp.where(o == t, depth_ref[...].astype(jnp.float32), depths[...].astype(jnp.float32))
         for w in range(NW):
             g_re = across_v[:, w * slots : (w + 1) * slots]
             g_im = across_v[:, (NW + w) * slots : (NW + w + 1) * slots]
             l_re, l_im = left[o, 2 * w], left[o, 2 * w + 1]
-            part_out[o, 2 * w : 2 * w + 1, :] = jnp.sum(l_re * g_re - l_im * g_im, axis=0, keepdims=True)
-            part_out[o, 2 * w + 1 : 2 * w + 2, :] = jnp.sum(
-                l_re * g_im + l_im * g_re, axis=0, keepdims=True
-            )
-        part_out[o, 2 * NW :, :] = jnp.zeros((8 - 2 * NW, slots), jnp.float32)
+            weight = weights[w : w + 1]
+            sums[0] += weight * jnp.sum(l_re * g_re - l_im * g_im, axis=0, keepdims=True)
+            sums[1] += weight * jnp.sum(l_re * g_im + l_im * g_re, axis=0, keepdims=True)
+        for c in range(2):
+            part_out[owners * c + o : owners * c + o + 1, :] = sums[c]
 
     part_copies = []
-    for d in range(1, plane_total):
-        other, peer = plane_peer(d)
+    for dz, dp, dt in offsets:
+        peer = (lax.rem(z + dz, subgrids), lax.rem(p + dp, pols), lax.rem(t + dt, owners))
+        k = (dz * pols + dp) * owners + dt
         part_copies.append(
-            remote(
-                part_out.at[lax.rem(other, owners)],
-                part_in.at[plane],
-                part_send.at[d],
-                part_recv.at[d],
-                peer,
-            )
+            remote(part_out, part_in.at[z, p, t], part_send.at[k], part_recv.at[k], peer)
         )
     for copy in part_copies:
         copy.start()
-    part_in[plane] = part_out[t]
-    observed_in[p] = observed_out[...]
-    for copy in observed_copies:
+    part_in[z, p, t] = part_out[...]
+
+    for copy in side_copies:
         copy.wait()
-    observed = observed_in[0]
-    for q in range(1, pols):
-        observed = observed + observed_in[q]
-    depth = depth_ref[...].astype(jnp.float32)
-    own_idents = idents[across]
-    gains = gains_ref[...]
-    for copy in ident_copies:
-        copy.wait()
-    names = jnp.concatenate([idents[d, 0:3] for d in range(across_total)], axis=1)
     own_count = grad_ref.shape[0]
     index = (z * pols + p) * owners + t
     mine = (index * own_count + lax.broadcasted_iota(jnp.int32, (own_count, 1), 0)).astype(
         jnp.float32
     )
-    first_here = jnp.where(mine == names[0:1], 1.0, 0.0)
-    second_here = jnp.where(mine == names[1:2], 1.0, 0.0)
     channel_ids = lax.broadcasted_iota(jnp.int32, (NCH, 1), 0).astype(jnp.float32)
-    onehot = jnp.where(channel_ids == names[2:3], 1.0, 0.0).astype(jnp.bfloat16)
+    first_here = [jnp.where(mine == side[d, 16:17], 1.0, 0.0) for d in range(across_total)]
+    second_here = [jnp.where(mine == side[d, 17:18], 1.0, 0.0) for d in range(across_total)]
+    onehot = jnp.concatenate(
+        [
+            jnp.where(channel_ids == side[d, 18:19], 1.0, 0.0).astype(jnp.bfloat16)
+            for d in range(across_total)
+        ],
+        axis=1,
+    )
+    column = lambda k: jnp.concatenate([side[d, k : k + 1] for d in range(across_total)], axis=0)
+    gains = [column(k) for k in range(8)]
+    observed = [column(8 + k) for k in range(8)]
+    alive = column(19)
     for copy in part_copies:
         copy.wait()
 
-    pred = []
-    per_pol = part_in.shape[0] // NPOL
-    for q in range(NPOL):
-        block = part_in[q * per_pol]
-        for o in range(1, per_pol):
-            block = block + part_in[q * per_pol + o]
-        pred.append(
-            tuple(
-                sum(depth[w : w + 1] * block[2 * w + c : 2 * w + c + 1] for w in range(NW))
-                for c in range(2)
+    pred = [
+        tuple(
+            sum(
+                jnp.concatenate(
+                    [
+                        part_in[y, q, o, owners * c : owners * (c + 1)]
+                        for y in range(subgrids)
+                    ],
+                    axis=0,
+                )
+                for o in range(owners)
             )
-        )
-    residual, leading, trailing = model_terms(
-        pred,
-        [observed[k : k + 1] for k in range(2 * NPOL)],
-        [gains[k : k + 1] for k in range(4)],
-        [gains[4 + k : 5 + k] for k in range(4)],
-        own_idents[3:4],
-    )
-    record_out[...] = jnp.concatenate(leading + trailing, axis=0)
-    record_copies = []
-    for d in range(1, across_total):
-        other, peer = across_peer(d)
-        record_copies.append(
-            remote(record_out, record_in.at[across], record_send.at[d], record_recv.at[d], peer)
-        )
-    for copy in record_copies:
-        copy.start()
-    record_in[across] = record_out[...]
-    rest = jnp.concatenate(residual, axis=0)
+            for c in range(2)
+        )
+        for q in range(NPOL)
+    ]
+    residual, leading, trailing = model_terms(pred, observed, gains[:4], gains[4:], alive)
+    for k in range(2 * NPOL):
+        rests[:, k : k + 1, :] = residual[k][:, None, :]
+    rest = rests[across]
     quarter = observed_ref.shape[1]
     own_rest = jnp.zeros((2 * NPOL, quarter), jnp.float32)
     for q in range(pols):
         own_rest = jnp.where(p == q, rest[:, q * quarter : (q + 1) * quarter], own_rest)
     residual_ref[...] = own_rest
-    for copy in record_copies:
-        copy.wait()
-
-    piece = jnp.concatenate([record_in[d] for d in range(across_total)], axis=1)
+
     weighted = jnp.concatenate(
         [
-            first_here * piece[k : k + 1] + second_here * piece[4 + k : 5 + k]
+            jnp.concatenate(
+                [
+                    first_here[d] * leading[k][d : d + 1]
+                    + second_here[d] * trailing[k][d : d + 1]
+                    for d in range(across_total)
+                ],
+                axis=1,
+            )
             for k in range(4)
         ],
         axis=0,
@@ -1066,7 +1073,7 @@
     vmem = pl.BlockSpec(memory_space=pltpu.VMEM)
     dma = lambda n: pltpu.SemaphoreType.DMA((n,))
     held = lambda a: pltpu.VMEM(a.shape, a.dtype)
-    across_total, plane_total = subgrids * owners, pols * owners
+    across_total, all_total = subgrids * owners, subgrids * pols * owners
     f32, bf16 = jnp.float32, jnp.bfloat16
     residual, grad = pl.pallas_call(
         functools.partial(fused_kernel, sizes),
@@ -1099,30 +1106,29 @@
             pltpu.VMEM((owners, 2 * NW * slots, 2 * SG), bf16),
             pltpu.VMEM((owners, 4, FGRID * rows, slots), f32),
             pltpu.VMEM((8, slots), f32),
-            pltpu.VMEM((across_total, 8, slots), f32),
-            pltpu.VMEM((owners, 8, slots), f32),
-            pltpu.VMEM((plane_total, 8, slots), f32),
+            pltpu.VMEM((8, slots), f32),
+            held(depth),
+            pltpu.VMEM((across_total, 20, slots), f32),
+            pltpu.VMEM((2 * owners, slots), f32),
+            pltpu.VMEM((subgrids, pols, owners, 2 * owners, slots), f32),
             pltpu.VMEM((8, slots), f32),
             pltpu.VMEM((pols, 8, slots), f32),
-            pltpu.VMEM((8, slots), f32),
             pltpu.VMEM((across_total, 8, slots), f32),
             dma(15),
             dma(chunks),
             dma(chunks * subgrids),
             dma(chunks * subgrids),
-            dma(2),
-            dma(2),
+            dma(3),
+            dma(3),
             dma(pols),
             dma(pols),
-            dma(plane_total),
-            dma(plane_total),
             dma(across_total),
             dma(across_total),
-            dma(across_total),
-            dma(across_total),
+            dma(all_total),
+            dma(all_total),
         ],
         compiler_params=pltpu.CompilerParams(
-            collective_id=0, has_side_effects=True, vmem_limit_bytes=56 << 20
+            collective_id=0, has_side_effects=True, vmem_limit_bytes=36 << 20
         ),
     )(*[pltpu.with_memory_space_constraint(a, pltpu.HBM) for a in operands])
     return pl.pallas_call(
@@ -1134,6 +1140,7 @@
         in_specs=[vmem] * 2,
         out_specs=[hbm] * 2,
         scratch_shapes=[dma(2)],
+        compiler_params=pltpu.CompilerParams(vmem_limit_bytes=1 << 20),
     )(residual, grad)
 
 

time: 32.4 us -> 30.1 us (0.929)
  Pallas kernels: 31.6 us -> 29.3 us
    pallas_call x1, Pallas kernels: 30.1 us -> 28.7 us  [fused(): pl.pallas_call(functools.partial(fused_kernel, sizes), out_shape=(jax.Sha...]
    pallas_call x1, Pallas kernels: 1.49 us -> 0.65 us  [fused(): pl.pallas_call(emit_kernel, out_shape=(jax.ShapeDtypeStruct(residual.shap...]
where the time goes in v2:
time: 30.1 us; the launch traced here: 30 us
  Pallas kernels  29.3 us (97%)
  between operations  0.64 us (2%)
    pallas_call x1, Pallas kernels, fused(): pl.pallas_call(functools.partial(fused_kernel, sizes), out_shape=(jax.Sha...  28.7 us
    pallas_call x1, Pallas kernels, fused(): pl.pallas_call(emit_kernel, out_shape=(jax.ShapeDtypeStruct(residual.shap...  0.65 us

profile of v2, /device:TPU:0, one launch (start us, length us, event | category | flops | bytes accessed | tf_op | source)
XLA Modules:
  0.0 30.0 jit_solution(12504400010970460106)
XLA Ops:
  0.6 28.7 %shard_map.167 = (f32[8,32]{1,0:T(8,128)S(1)}, f32[16,1024]{1,0:T(8,128)S(1)}) custom-call(s32[3,1,8]{2,1,0:T(1,128)} %bitcast.17, s32[1022,2,128]{2,1,0:T(2,128)} %bitcast.13, f32[256,4,512]{2,1,0:T(4,128)} %gain_hbm.1, f32[64,512]{1,0:T(8,128)} %constant.19.clone.p_hbm, f32[64,512]{1,0:T(8,128)} %constant.20.clone.q_hbm, f32[64,512]{1,0:T(8,128)} %constant.21.clone.c_hbm, ...), custom_call_target="tpu_custom_call" | custom-call | tf_op jit(solution)/shard_map/pallas_call | solution.py:1078
  29.3 0.7 %shard_map.168 = (f32[8,32]{1,0:T(8,128)}, f32[16,1024]{1,0:T(8,128)}) custom-call(f32[8,32]{1,0:T(8,128)S(1)} %get-tuple-element.6.residual_ref, f32[16,1024]{1,0:T(8,128)S(1)} %get-tuple-element.7.grad_ref), custom_call_target="tpu_custom_call" | custom-call | tf_op jit(solution)/shard_map/pallas_call | solution.py:1134

commit v3 on v2

--- a/solution.py
+++ b/solution.py
@@ -19,6 +19,7 @@
 NST = 512
 CHUNK = 1024
 PIECES = 2
+FORWARD = 2
 
 w_chirp = 0.37
 grad_scale = 0.1
@@ -683,9 +684,8 @@
     c_ref,
     s_ref,
     x_ref,
-    lead_ref,
-    trail_ref,
-    depth_ref,
+    tapers,
+    depths,
     observed_ref,
     table_ref,
     second_ref,
@@ -693,12 +693,10 @@
     factors,
     contrib,
     got,
-    tapers,
     right,
     left,
     gains_ref,
     idents_ref,
-    depths,
     side,
     part_out,
     part_in,
@@ -707,10 +705,16 @@
     rests,
     load_sem,
     chunk_sem,
-    got_send,
-    got_recv,
-    taper_send,
-    taper_recv,
+    pair_send,
+    pair_recv,
+    chip_send,
+    chip_recv,
+    relay_send,
+    relay_recv,
+    far_send,
+    far_recv,
+    near_send,
+    near_recv,
     observed_send,
     observed_recv,
     side_send,
@@ -720,9 +724,14 @@
 ):
     subgrids, pols, owners = sizes
     z, p, t = lax.axis_index("facet"), lax.axis_index("pol"), lax.axis_index("tm")
-    slots = lead_ref.shape[0]
+    _, _, slots, _ = tapers.shape
     facets, _, rows, length = x_ref.shape
-    _, groups, _, width = contrib.shape
+    _, _, groups, _, width = contrib.shape
+    side_z, own = lax.rem(z, 2), z // 2
+    far = 1 - own
+    pair_z = z + 1 - 2 * side_z
+    far_z = z + 2 - 4 * own
+    partner = lax.rem(t + 1, owners)
     mesh_id = pl.DeviceIdType.MESH
 
     def remote(src, dst, send, recv, peer):
@@ -772,14 +781,14 @@
         (s_hbm, s_ref),
         (p_hbm, p_ref),
         (q_hbm, q_ref),
-        (lead_hbm, lead_ref),
-        (trail_hbm, trail_ref),
-        (depth_hbm, depth_ref),
+        (trail_hbm, tapers.at[own, 0]),
+        (lead_hbm, tapers.at[own, 1]),
+        (depth_hbm, depths.at[own]),
         (observed_hbm, observed_ref),
         (chirp_hbm, chirp_ref),
         (second_hbm, second_ref),
-        (table_re_hbm.at[:, t], table_ref.at[0]),
-        (table_im_hbm.at[:, t], table_ref.at[1]),
+        (table_re_hbm.at[pl.ds(own * 2 * groups, 2 * groups)], table_ref.at[0]),
+        (table_im_hbm.at[pl.ds(own * 2 * groups, 2 * groups)], table_ref.at[1]),
         (block_hbm, block_ref),
         (links_hbm, links_ref),
         (gain_hbm, gain_ref),
@@ -806,11 +815,56 @@
             p_ref[part : part + 1, :] * cosine + q_ref[part : part + 1, :] * sine
         ).astype(jnp.bfloat16)
 
+    for copy in loads[4:9]:
+        copy.wait()
+    quarter = observed_ref.shape[1]
+    place = lax.broadcasted_iota(jnp.int32, (2 * NPOL, slots), 1)
+    observed_out[...] = jnp.where(
+        (place >= p * quarter) & (place < (p + 1) * quarter),
+        jnp.concatenate([observed_ref[...]] * pols, axis=1),
+        0.0,
+    )
+    pl.semaphore_wait(barrier, across_total - 1 + (pols - 1) * owners)
+    share = lambda q: pl.ds(pl.multiple_of(q * quarter, quarter), quarter)
+    far_copies = [
+        remote(
+            tapers.at[own, :, share(q)],
+            tapers.at[own, :, share(q)],
+            far_send.at[k],
+            far_recv.at[k],
+            (far_z, p, t),
+        )
+        for k, q in enumerate((p, pols - 1 - p))
+    ]
+    far_copies.append(
+        remote(depths.at[own], depths.at[own], far_send.at[2], far_recv.at[2], (far_z, p, t))
+    )
+    observed_copies = []
+    for d in range(1, pols):
+        q = lax.rem(p + d, pols)
+        observed_copies.append(
+            remote(
+                observed_out, observed_in.at[p], observed_send.at[d], observed_recv.at[d], (z, q, t)
+            )
+        )
+    for copy in far_copies + observed_copies:
+        copy.start()
+    across_x = p + 1 - 2 * lax.rem(p, 2)
+    near_copies = [
+        remote(
+            tapers.at[far, :, share(p)],
+            tapers.at[far, :, share(p)],
+            near_send.at[k],
+            near_recv.at[k],
+            (z, q, t),
+        )
+        for k, q in enumerate((across_x, pols - 1 - across_x))
+    ]
+
     lane = lax.broadcasted_iota(jnp.int32, (rows, 2 * MC), 1)
     sign = jnp.where(lane < MC, -1.0, 1.0)
     part_width = width // PIECES
-    partner = lax.rem(t + 1, owners)
-    copies, taper_copies, observed_copies = [], [], []
+    pair_copies, chip_copies, relay_copies = [], [], []
     for c in range(chunks):
         x_loads[c].wait()
         x = x_ref[c * per_chunk : (c + 1) * per_chunk].reshape(per_chunk * 2 * rows, length)
@@ -822,58 +876,47 @@
                 first = total[2 * f * rows : (2 * f + 1) * rows, cut]
                 second = total[(2 * f + 1) * rows : (2 * f + 2) * rows, cut]
                 j = piece * per_chunk + f
-                contrib[s, group, :, j * 2 * MC : (j + 1) * 2 * MC] = (
+                contrib[s % 2, s // 2, group, :, j * 2 * MC : (j + 1) * 2 * MC] = (
                     first + sign * pltpu.roll(second, MC, 1)
                 ).astype(jnp.bfloat16)
-        if c == 0:
-            pl.semaphore_wait(barrier, across_total - 1 + (pols - 1) * owners)
         lanes = pl.ds(piece * part_width, part_width)
-        for d in sorted(range(1, subgrids), key=lambda d: -min(d, subgrids - d)):
-            other = lax.rem(z + d, subgrids)
-            copy = remote(
-                contrib.at[other, group, :, lanes],
-                got.at[z, group, :, lanes],
-                got_send.at[c * subgrids + d],
-                got_recv.at[c * subgrids + d],
-                (other, p, t),
+        pair_copies.append(
+            remote(
+                contrib.at[1 - side_z, :, group, :, lanes],
+                got.at[:, side_z, group, t, :, lanes],
+                pair_send.at[c],
+                pair_recv.at[c],
+                (pair_z, p, t),
             )
-            copy.start()
-            copies.append(copy)
-        if c == 0:
-            for copy in loads[4:9]:
-                copy.wait()
-            taper_copies = [
-                remote(src, dst, taper_send.at[k], taper_recv.at[k], (z, p, partner))
-                for k, (src, dst) in enumerate(
-                    [
-                        (trail_ref, tapers.at[0]),
-                        (lead_ref, tapers.at[1]),
-                        (depth_ref, depths),
-                    ]
-                )
-            ]
-            quarter = observed_ref.shape[1]
-            place = lax.broadcasted_iota(jnp.int32, (2 * NPOL, slots), 1)
-            observed_out[...] = jnp.where(
-                (place >= p * quarter) & (place < (p + 1) * quarter),
-                jnp.concatenate([observed_ref[...]] * pols, axis=1),
-                0.0,
+        )
+        chip_copies.append(
+            remote(
+                contrib.at[side_z, :, group, :, lanes],
+                got.at[:, side_z, group, t, :, lanes],
+                chip_send.at[c],
+                chip_recv.at[c],
+                (z, p, partner),
             )
-            for d in range(1, pols):
-                q = lax.rem(p + d, pols)
-                observed_copies.append(
-                    remote(
-                        observed_out,
-                        observed_in.at[p],
-                        observed_send.at[d],
-                        observed_recv.at[d],
-                        (z, q, t),
-                    )
-                )
-            for copy in taper_copies + observed_copies:
+        )
+        relay_copies.append(
+            remote(
+                got.at[:, 1 - side_z, group, t, :, lanes],
+                got.at[:, 1 - side_z, group, t, :, lanes],
+                relay_send.at[c],
+                relay_recv.at[c],
+                (z, p, partner),
+            )
+        )
+        pair_copies[c].start()
+        chip_copies[c].start()
+        if c == chunks - FORWARD:
+            far_copies[0].wait_recv()
+            for copy in near_copies:
                 copy.start()
 
-    got[z] = contrib[z]
+    for k in range(2):
+        for group in range(groups):
+            got[k, side_z, group, t] = contrib[side_z, k, group]
     for copy in loads[9:]:
         copy.wait()
     gather_lookups(block_ref, links_ref, gain_ref, gains_ref, idents_ref)
@@ -895,14 +938,15 @@
     for copy in side_copies:
         copy.start()
 
-    table_re = jnp.concatenate([table_ref[0, i] for i in range(FGRID)], axis=0)
-    table_im = jnp.concatenate([table_ref[1, i] for i in range(FGRID)], axis=0)
+    span = 2 * groups * owners * rows
+    table_re = table_ref[0].reshape(span, SG)
+    table_im = table_ref[1].reshape(span, SG)
     turn = jnp.where(
         lax.broadcasted_iota(jnp.int32, (3 * slots, 2 * MC), 1) < MC, -1.0, 1.0
     )
 
-    def prepare(owner, trail, lead):
-        trail3 = chirped_rows(trail, chirp_ref)
+    def prepare(k):
+        trail3 = chirped_rows(tapers[k, 0], chirp_ref)
         a = jnp.dot(trail3, second_ref[...], preferred_element_type=jnp.float32)
         b = jnp.concatenate(
             [
@@ -912,38 +956,42 @@
             axis=1,
         )
         n0, n1, n2 = slice(0, slots), slice(slots, 2 * slots), slice(2 * slots, 3 * slots)
-        right[owner, 0:slots, :] = a[n0].astype(jnp.bfloat16)
-        right[owner, slots : 2 * slots, :] = (a[n1] - b[n2]).astype(jnp.bfloat16)
-        right[owner, 2 * slots : 3 * slots, :] = b[n0].astype(jnp.bfloat16)
-        right[owner, 3 * slots : 4 * slots, :] = (b[n1] + a[n2]).astype(jnp.bfloat16)
-        lead3 = chirped_rows(lead, chirp_ref)
+        right[k, 0:slots, :] = a[n0].astype(jnp.bfloat16)
+        right[k, slots : 2 * slots, :] = (a[n1] - b[n2]).astype(jnp.bfloat16)
+        right[k, 2 * slots : 3 * slots, :] = b[n0].astype(jnp.bfloat16)
+        right[k, 3 * slots : 4 * slots, :] = (b[n1] + a[n2]).astype(jnp.bfloat16)
+        lead3 = chirped_rows(tapers[k, 1], chirp_ref)
         u = nt_dot(table_re, lead3)
         v = nt_dot(table_im, lead3)
-        left[owner, 0] = u[:, n0]
-        left[owner, 1] = v[:, n0]
-        left[owner, 2] = u[:, n1] - v[:, n2]
-        left[owner, 3] = u[:, n2] + v[:, n1]
-
-    prepare(t, trail_ref[...], lead_ref[...])
-    for copy in taper_copies:
+        left[k, 0] = u[:, n0]
+        left[k, 1] = v[:, n0]
+        left[k, 2] = u[:, n1] - v[:, n2]
+        left[k, 3] = u[:, n2] + v[:, n1]
+
+    prepare(own)
+    for pair, relay in zip(pair_copies, relay_copies):
+        pair.wait_recv()
+        relay.start()
+    for copy in far_copies[1:] + near_copies:
+        copy.wait_recv()
+    prepare(far)
+    for copy in side_copies + chip_copies + relay_copies:
         copy.wait()
-    prepare(partner, tapers[0], tapers[1])
-    for copy in copies:
-        copy.wait()
-    whole = got[...].reshape(subgrids * groups * rows, width)
-    for o in range(owners):
-        across_v = nt_dot(whole, right[o])
+    for copy in pair_copies + far_copies + near_copies:
+        copy.wait_send()
+    for k in range(2):
+        spread_v = nt_dot(got[k].reshape(span, width), right[k])
+        weights = depths[k].astype(jnp.float32)
         sums = [0.0, 0.0]
-        weights = jnp.where(o == t, depth_ref[...].astype(jnp.float32), depths[...].astype(jnp.float32))
         for w in range(NW):
-            g_re = across_v[:, w * slots : (w + 1) * slots]
-            g_im = across_v[:, (NW + w) * slots : (NW + w + 1) * slots]
-            l_re, l_im = left[o, 2 * w], left[o, 2 * w + 1]
+            g_re = spread_v[:, w * slots : (w + 1) * slots]
+            g_im = spread_v[:, (NW + w) * slots : (NW + w + 1) * slots]
+            l_re, l_im = left[k, 2 * w], left[k, 2 * w + 1]
             weight = weights[w : w + 1]
             sums[0] += weight * jnp.sum(l_re * g_re - l_im * g_im, axis=0, keepdims=True)
             sums[1] += weight * jnp.sum(l_re * g_im + l_im * g_re, axis=0, keepdims=True)
         for c in range(2):
-            part_out[owners * c + o : owners * c + o + 1, :] = sums[c]
+            part_out[2 * c + k : 2 * c + k + 1, :] = sums[c]
 
     part_copies = []
     for dz, dp, dt in offsets:
@@ -956,8 +1004,6 @@
         copy.start()
     part_in[z, p, t] = part_out[...]
 
-    for copy in side_copies:
-        copy.wait()
     own_count = grad_ref.shape[0]
     index = (z * pols + p) * owners + t
     mine = (index * own_count + lax.broadcasted_iota(jnp.int32, (own_count, 1), 0)).astype(
@@ -980,27 +1026,26 @@
     for copy in part_copies:
         copy.wait()
 
-    pred = [
-        tuple(
-            sum(
+    pred = []
+    for q in range(NPOL):
+        both = [[part_in[y, q, o] + part_in[y + 2, q, o] for o in range(owners)] for y in range(2)]
+        pred.append(
+            tuple(
                 jnp.concatenate(
                     [
-                        part_in[y, q, o, owners * c : owners * (c + 1)]
-                        for y in range(subgrids)
+                        both[s % 2][o][2 * c + s // 2 : 2 * c + s // 2 + 1]
+                        for s in range(subgrids)
+                        for o in range(owners)
                     ],
                     axis=0,
                 )
-                for o in range(owners)
+                for c in range(2)
             )
-            for c in range(2)
-        )
-        for q in range(NPOL)
-    ]
+        )
     residual, leading, trailing = model_terms(pred, observed, gains[:4], gains[4:], alive)
     for k in range(2 * NPOL):
         rests[:, k : k + 1, :] = residual[k][:, None, :]
     rest = rests[across]
-    quarter = observed_ref.shape[1]
     own_rest = jnp.zeros((2 * NPOL, quarter), jnp.float32)
     for q in range(pols):
         own_rest = jnp.where(p == q, rest[:, q * quarter : (q + 1) * quarter], own_rest)
@@ -1092,34 +1137,37 @@
             pltpu.VMEM((spread, width), f32),
             pltpu.VMEM((spread, width), f32),
             held(x),
-            held(lead),
-            held(trail),
-            held(depth),
+            pltpu.VMEM((2, 2, slots, SG), bf16),
+            pltpu.VMEM((2,) + depth.shape, bf16),
             held(observed),
-            pltpu.VMEM((2, FGRID, rows, SG), bf16),
+            pltpu.VMEM((2, 2 * groups, owners, rows, SG), bf16),
             pltpu.VMEM((SG, 2 * SG), bf16),
             pltpu.VMEM((2, SG), f32),
             pltpu.VMEM((length, width), bf16),
-            pltpu.VMEM((subgrids, groups, rows, 2 * SG), bf16),
-            pltpu.VMEM((subgrids, groups, rows, 2 * SG), bf16),
-            pltpu.VMEM((2, slots, SG), bf16),
-            pltpu.VMEM((owners, 2 * NW * slots, 2 * SG), bf16),
-            pltpu.VMEM((owners, 4, FGRID * rows, slots), f32),
+            pltpu.VMEM((2, 2, groups, rows, 2 * SG), bf16),
+            pltpu.VMEM((2, 2, groups, owners, rows, 2 * SG), bf16),
+            pltpu.VMEM((2, 2 * NW * slots, 2 * SG), bf16),
+            pltpu.VMEM((2, 4, 2 * groups * owners * rows, slots), f32),
             pltpu.VMEM((8, slots), f32),
             pltpu.VMEM((8, slots), f32),
-            held(depth),
             pltpu.VMEM((across_total, 20, slots), f32),
-            pltpu.VMEM((2 * owners, slots), f32),
-            pltpu.VMEM((subgrids, pols, owners, 2 * owners, slots), f32),
+            pltpu.VMEM((4, slots), f32),
+            pltpu.VMEM((subgrids, pols, owners, 4, slots), f32),
             pltpu.VMEM((8, slots), f32),
             pltpu.VMEM((pols, 8, slots), f32),
             pltpu.VMEM((across_total, 8, slots), f32),
             dma(15),
             dma(chunks),
-            dma(chunks * subgrids),
-            dma(chunks * subgrids),
+            dma(chunks),
+            dma(chunks),
+            dma(chunks),
+            dma(chunks),
+            dma(chunks),
+            dma(chunks),
             dma(3),
             dma(3),
+            dma(2),
+            dma(2),
             dma(pols),
             dma(pols),
             dma(across_total),
@@ -1163,7 +1211,7 @@
     block_table = visibility_groups_table.reshape(3, visibility_groups_table.shape[3])
     observed = measured_correlations.reshape(2 * NPOL, quarter)
 
-    if tile_spectral_lines.shape[0] % FGRID == 0:
+    if tile_spectral_lines.shape[0] % FGRID == 0 and sizes == (4, NPOL, 2):
         table_re, table_im, second = [jnp.asarray(t) for t in subgrid_tables()]
         own_count = NST // (subgrids * pols * owners)
         residual, gain_grad = fused(

time: 30.1 us -> 28.5 us (0.947)
  Pallas kernels: 29.3 us -> 27.7 us
    pallas_call x1, Pallas kernels: 28.7 us -> 27 us  [fused(): pl.pallas_call(functools.partial(fused_kernel, sizes), out_shape=(jax.Sha...]
where the time goes in v3:
time: 28.5 us; the launch traced here: 28.3 us
  Pallas kernels  27.7 us (97%)
  between operations  0.64 us (2%)
    pallas_call x1, Pallas kernels, fused(): pl.pallas_call(functools.partial(fused_kernel, sizes), out_shape=(jax.Sha...  27 us
    pallas_call x1, Pallas kernels, fused(): pl.pallas_call(emit_kernel, out_shape=(jax.ShapeDtypeStruct(residual.shap...  0.65 us

profile of v3, /device:TPU:0, one launch (start us, length us, event | category | flops | bytes accessed | tf_op | source)
XLA Modules:
  0.0 28.3 jit_solution(5507359006273168641)
XLA Ops:
  0.6 27.0 %shard_map.167 = (f32[8,32]{1,0:T(8,128)S(1)}, f32[16,1024]{1,0:T(8,128)S(1)}) custom-call(s32[3,1,8]{2,1,0:T(1,128)} %bitcast.17, s32[1022,2,128]{2,1,0:T(2,128)} %bitcast.13, f32[256,4,512]{2,1,0:T(4,128)} %gain_hbm.1, f32[64,512]{1,0:T(8,128)} %constant.19.clone.p_hbm, f32[64,512]{1,0:T(8,128)} %constant.20.clone.q_hbm, f32[64,512]{1,0:T(8,128)} %constant.21.clone.c_hbm, ...), custom_call_target="tpu_custom_call" | custom-call | tf_op jit(solution)/shard_map/pallas_call | solution.py:1123
  27.7 0.7 %shard_map.168 = (f32[8,32]{1,0:T(8,128)}, f32[16,1024]{1,0:T(8,128)}) custom-call(f32[8,32]{1,0:T(8,128)S(1)} %get-tuple-element.6.residual_ref, f32[16,1024]{1,0:T(8,128)S(1)} %get-tuple-element.7.grad_ref), custom_call_target="tpu_custom_call" | custom-call | tf_op jit(solution)/shard_map/pallas_call | solution.py:1182

commit v4 on v3

--- a/solution.py
+++ b/solution.py
@@ -19,7 +19,7 @@
 NST = 512
 CHUNK = 1024
 PIECES = 2
-FORWARD = 2
+FORWARD = 1
 
 w_chirp = 0.37
 grad_scale = 0.1
@@ -828,13 +828,13 @@
     share = lambda q: pl.ds(pl.multiple_of(q * quarter, quarter), quarter)
     far_copies = [
         remote(
-            tapers.at[own, :, share(q)],
-            tapers.at[own, :, share(q)],
-            far_send.at[k],
-            far_recv.at[k],
+            tapers.at[own, side, share(p)],
+            tapers.at[own, side, share(p)],
+            far_send.at[side],
+            far_recv.at[side],
             (far_z, p, t),
         )
-        for k, q in enumerate((p, pols - 1 - p))
+        for side in range(2)
     ]
     far_copies.append(
         remote(depths.at[own], depths.at[own], far_send.at[2], far_recv.at[2], (far_z, p, t))
@@ -849,17 +849,24 @@
         )
     for copy in far_copies + observed_copies:
         copy.start()
-    across_x = p + 1 - 2 * lax.rem(p, 2)
+    others = pols - 1
     near_copies = [
         remote(
-            tapers.at[far, :, share(p)],
-            tapers.at[far, :, share(p)],
-            near_send.at[k],
-            near_recv.at[k],
-            (z, q, t),
-        )
-        for k, q in enumerate((across_x, pols - 1 - across_x))
+            tapers.at[far, side, share(p)],
+            tapers.at[far, side, share(p)],
+            near_send.at[others * side + d - 1],
+            near_recv.at[others * side + d - 1],
+            (z, lax.rem(p + d, pols), t),
+        )
+        for side in range(2)
+        for d in (2, 1, 3)
     ]
+
+    def forward(side):
+        far_copies[side].wait_recv()
+        for copy in near_copies[others * side : others * side + others]:
+            copy.start()
+
 
     lane = lax.broadcasted_iota(jnp.int32, (rows, 2 * MC), 1)
     sign = jnp.where(lane < MC, -1.0, 1.0)
@@ -910,9 +917,7 @@
         pair_copies[c].start()
         chip_copies[c].start()
         if c == chunks - FORWARD:
-            far_copies[0].wait_recv()
-            for copy in near_copies:
-                copy.start()
+            forward(0)
 
     for k in range(2):
         for group in range(groups):
@@ -937,6 +942,7 @@
         )
     for copy in side_copies:
         copy.start()
+    forward(1)
 
     span = 2 * groups * owners * rows
     table_re = table_ref[0].reshape(span, SG)
@@ -945,7 +951,7 @@
         lax.broadcasted_iota(jnp.int32, (3 * slots, 2 * MC), 1) < MC, -1.0, 1.0
     )
 
-    def prepare(k):
+    def prepare_right(k):
         trail3 = chirped_rows(tapers[k, 0], chirp_ref)
         a = jnp.dot(trail3, second_ref[...], preferred_element_type=jnp.float32)
         b = jnp.concatenate(
@@ -960,6 +966,9 @@
         right[k, slots : 2 * slots, :] = (a[n1] - b[n2]).astype(jnp.bfloat16)
         right[k, 2 * slots : 3 * slots, :] = b[n0].astype(jnp.bfloat16)
         right[k, 3 * slots : 4 * slots, :] = (b[n1] + a[n2]).astype(jnp.bfloat16)
+
+    def prepare_left(k):
+        n0, n1, n2 = slice(0, slots), slice(slots, 2 * slots), slice(2 * slots, 3 * slots)
         lead3 = chirped_rows(tapers[k, 1], chirp_ref)
         u = nt_dot(table_re, lead3)
         v = nt_dot(table_im, lead3)
@@ -968,17 +977,21 @@
         left[k, 2] = u[:, n1] - v[:, n2]
         left[k, 3] = u[:, n2] + v[:, n1]
 
-    prepare(own)
-    for pair, relay in zip(pair_copies, relay_copies):
+    prepare_right(own)
+    prepare_left(own)
+    for pair, relay in zip(pair_copies[:-1], relay_copies[:-1]):
         pair.wait_recv()
         relay.start()
-    for copy in far_copies[1:] + near_copies:
+    for copy in near_copies[:others]:
         copy.wait_recv()
-    prepare(far)
-    for copy in side_copies + chip_copies + relay_copies:
+    prepare_right(far)
+    pair_copies[-1].wait_recv()
+    relay_copies[-1].start()
+    for copy in [far_copies[2]] + near_copies[others:]:
+        copy.wait_recv()
+    prepare_left(far)
+    for copy in chip_copies + relay_copies:
         copy.wait()
-    for copy in pair_copies + far_copies + near_copies:
-        copy.wait_send()
     for k in range(2):
         spread_v = nt_dot(got[k].reshape(span, width), right[k])
         weights = depths[k].astype(jnp.float32)
@@ -1003,6 +1016,10 @@
     for copy in part_copies:
         copy.start()
     part_in[z, p, t] = part_out[...]
+    for copy in pair_copies + far_copies + near_copies:
+        copy.wait_send()
+    for copy in side_copies:
+        copy.wait()
 
     own_count = grad_ref.shape[0]
     index = (z * pols + p) * owners + t
@@ -1166,8 +1183,8 @@
             dma(chunks),
             dma(3),
             dma(3),
-            dma(2),
-            dma(2),
+            dma(2 * pols - 2),
+            dma(2 * pols - 2),
             dma(pols),
             dma(pols),
             dma(across_total),

time: 28.5 us -> 26.6 us (0.933)
  Pallas kernels: 27.7 us -> 25.8 us
    pallas_call x1, Pallas kernels: 27 us -> 25.1 us  [fused(): pl.pallas_call(functools.partial(fused_kernel, sizes), out_shape=(jax.Sha...]
where the time goes in v4:
time: 26.6 us; the launch traced here: 26.4 us
  Pallas kernels  25.8 us (97%)
  between operations  0.64 us (2%)
    pallas_call x1, Pallas kernels, fused(): pl.pallas_call(functools.partial(fused_kernel, sizes), out_shape=(jax.Sha...  25.1 us
    pallas_call x1, Pallas kernels, fused(): pl.pallas_call(emit_kernel, out_shape=(jax.ShapeDtypeStruct(residual.shap...  0.65 us

profile of v4, /device:TPU:0, one launch (start us, length us, event | category | flops | bytes accessed | tf_op | source)
XLA Modules:
  0.0 26.4 jit_solution(3651044873489623436)
XLA Ops:
  0.6 25.1 %shard_map.167 = (f32[8,32]{1,0:T(8,128)S(1)}, f32[16,1024]{1,0:T(8,128)S(1)}) custom-call(s32[3,1,8]{2,1,0:T(1,128)} %bitcast.17, s32[1022,2,128]{2,1,0:T(2,128)} %bitcast.13, f32[256,4,512]{2,1,0:T(4,128)} %gain_hbm.1, f32[64,512]{1,0:T(8,128)} %constant.19.clone.p_hbm, f32[64,512]{1,0:T(8,128)} %constant.20.clone.q_hbm, f32[64,512]{1,0:T(8,128)} %constant.21.clone.c_hbm, ...), custom_call_target="tpu_custom_call" | custom-call | tf_op jit(solution)/shard_map/pallas_call | solution.py:1140
  25.8 0.7 %shard_map.168 = (f32[8,32]{1,0:T(8,128)}, f32[16,1024]{1,0:T(8,128)}) custom-call(f32[8,32]{1,0:T(8,128)S(1)} %get-tuple-element.6.residual_ref, f32[16,1024]{1,0:T(8,128)S(1)} %get-tuple-element.7.grad_ref), custom_call_target="tpu_custom_call" | custom-call | tf_op jit(solution)/shard_map/pallas_call | solution.py:1199

commit v5 on v4

--- a/solution.py
+++ b/solution.py
@@ -19,7 +19,7 @@
 NST = 512
 CHUNK = 1024
 PIECES = 2
-FORWARD = 1
+FORWARD = 2
 
 w_chirp = 0.37
 grad_scale = 0.1
@@ -600,6 +600,23 @@
             collective_id=0, has_side_effects=True, vmem_limit_bytes=48 << 20
         ),
     )(*operands)
+
+
+def folded_factors(subgrids):
+    half = lambda odd, s, c: [s * 2 * MC + c * MC + k for k in range(odd, MC, 2)]
+    order = []
+    for odd in range(2):
+        for first in range(0, subgrids, 2):
+            for c in range(2):
+                for s in ((first + 1, first) if odd else (first, first + 1)):
+                    order += half(odd, s, c)
+    p, q, cosine, sine = [t[:, order] for t in fourier_factors(subgrids)]
+    return p[: len(p) // 2], q[: len(q) // 2], cosine, sine
+
+
+def folded_second(second):
+    split = second.reshape(SG, 2 * FGRID, MC // 2, 2)
+    return np.concatenate([split[..., 0], split[..., 1]], axis=2).reshape(SG, 2 * SG)
 
 
 def gather_lookups(block_ref, links_ref, gain_ref, gains_ref, idents_ref):
@@ -810,7 +827,8 @@
         copy.wait()
     spread = c_ref.shape[0]
     cosine, sine = c_ref[...], s_ref[...]
-    for part in range(length // spread):
+    half = length // 2
+    for part in range(half // spread):
         factors[part * spread : (part + 1) * spread, :] = (
             p_ref[part : part + 1, :] * cosine + q_ref[part : part + 1, :] * sine
         ).astype(jnp.bfloat16)
@@ -870,22 +888,42 @@
 
     lane = lax.broadcasted_iota(jnp.int32, (rows, 2 * MC), 1)
     sign = jnp.where(lane < MC, -1.0, 1.0)
+    front = lane % MC < MC // 2
+    folded = factors.shape[1] // 2
     part_width = width // PIECES
     pair_copies, chip_copies, relay_copies = [], [], []
     for c in range(chunks):
         x_loads[c].wait()
         x = x_ref[c * per_chunk : (c + 1) * per_chunk].reshape(per_chunk * 2 * rows, length)
-        total = jnp.dot(x, factors[...], preferred_element_type=jnp.float32)
+        totals = [
+            jnp.dot(
+                x[:, :half] + x[:, half:], factors[:, :folded], preferred_element_type=jnp.float32
+            ),
+            jnp.dot(
+                x[:, :half] - x[:, half:], factors[:, folded:], preferred_element_type=jnp.float32
+            ),
+        ]
         group, piece = c // PIECES, c % PIECES
-        for s in range(subgrids):
-            cut = slice(s * 2 * MC, (s + 1) * 2 * MC)
+        for pair in range(subgrids // 2):
+            cut = slice(pair * 2 * MC, (pair + 1) * 2 * MC)
             for f in range(per_chunk):
-                first = total[2 * f * rows : (2 * f + 1) * rows, cut]
-                second = total[(2 * f + 1) * rows : (2 * f + 2) * rows, cut]
-                j = piece * per_chunk + f
-                contrib[s % 2, s // 2, group, :, j * 2 * MC : (j + 1) * 2 * MC] = (
-                    first + sign * pltpu.roll(second, MC, 1)
-                ).astype(jnp.bfloat16)
+                even, odd = [
+                    total[2 * f * rows : (2 * f + 1) * rows, cut]
+                    + sign
+                    * pltpu.roll(total[(2 * f + 1) * rows : (2 * f + 2) * rows, cut], MC, 1)
+                    for total in totals
+                ]
+                place = slice(
+                    (piece * per_chunk + f) * 2 * MC, (piece * per_chunk + f + 1) * 2 * MC
+                )
+                contrib[0, pair, group, :, place] = jnp.where(front, even, odd).astype(jnp.bfloat16)
+                other = jnp.where(front, odd, even)
+                other = jnp.where(
+                    front,
+                    pltpu.roll(other, 2 * MC - MC // 2, 1),
+                    pltpu.roll(other, MC // 2, 1),
+                )
+                contrib[1, pair, group, :, place] = other.astype(jnp.bfloat16)
         lanes = pl.ds(piece * part_width, part_width)
         pair_copies.append(
             remote(
@@ -1084,7 +1122,8 @@
     )
     high = weighted.astype(jnp.bfloat16)
     low = (weighted - high.astype(jnp.float32)).astype(jnp.bfloat16)
-    summed = nt_dot(high, onehot) + nt_dot(low, onehot)
+    summed = nt_dot(jnp.concatenate([high, low], axis=0), onehot)
+    summed = summed[: high.shape[0]] + summed[high.shape[0] :]
     lane_group = lax.broadcasted_iota(jnp.int32, (own_count, 128), 1) // 32
     mixed = []
     for g in range(NCH // 32):
@@ -1149,8 +1188,8 @@
             pltpu.SMEM(block_table.shape, jnp.int32),
             held(links),
             held(gains),
-            pltpu.VMEM((length // spread, width), f32),
-            pltpu.VMEM((length // spread, width), f32),
+            pltpu.VMEM((length // 2 // spread, width), f32),
+            pltpu.VMEM((length // 2 // spread, width), f32),
             pltpu.VMEM((spread, width), f32),
             pltpu.VMEM((spread, width), f32),
             held(x),
@@ -1160,7 +1199,7 @@
             pltpu.VMEM((2, 2 * groups, owners, rows, SG), bf16),
             pltpu.VMEM((SG, 2 * SG), bf16),
             pltpu.VMEM((2, SG), f32),
-            pltpu.VMEM((length, width), bf16),
+            pltpu.VMEM((length // 2, width), bf16),
             pltpu.VMEM((2, 2, groups, rows, 2 * SG), bf16),
             pltpu.VMEM((2, 2, groups, owners, rows, 2 * SG), bf16),
             pltpu.VMEM((2, 2 * NW * slots, 2 * SG), bf16),
@@ -1229,7 +1268,7 @@
     observed = measured_correlations.reshape(2 * NPOL, quarter)
 
     if tile_spectral_lines.shape[0] % FGRID == 0 and sizes == (4, NPOL, 2):
-        table_re, table_im, second = [jnp.asarray(t) for t in subgrid_tables()]
+        table_re, table_im = [jnp.asarray(t) for t in subgrid_tables()[:2]]
         own_count = NST // (subgrids * pols * owners)
         residual, gain_grad = fused(
             sizes,
@@ -1237,7 +1276,7 @@
             visibility_groups_table.reshape(3, 1, visibility_groups_table.shape[3]),
             jnp.transpose(antenna_links.reshape(2, -1, 128), (1, 0, 2)),
             complex_receiver_factors,
-            *[jnp.asarray(t) for t in fourier_factors(subgrids)],
+            *[jnp.asarray(t) for t in folded_factors(subgrids)],
             tile_spectral_lines[:, 0],
             taper_leading_axis.reshape(slots, SG),
             taper_trailing_axis.reshape(slots, SG),
@@ -1245,7 +1284,7 @@
             observed,
             table_re.reshape(FGRID, owners, rows, SG),
             table_im.reshape(FGRID, owners, rows, SG),
-            second,
+            jnp.asarray(folded_second(subgrid_tables()[2])),
             jnp.asarray(np.stack(chirp_line())),
         )
         return residual.reshape(1, 2 * NPOL, 1, quarter), gain_grad

time: 26.6 us -> 25.9 us (0.974)
  Pallas kernels: 25.8 us -> 25.1 us
    pallas_call x1, Pallas kernels: 25.1 us -> 24.4 us  [fused(): pl.pallas_call(functools.partial(fused_kernel, sizes), out_shape=(jax.Sha...]
where the time goes in v5:
time: 25.9 us; the launch traced here: 25.7 us
  Pallas kernels  25.1 us (97%)
  between operations  0.64 us (2%)
    pallas_call x1, Pallas kernels, fused(): pl.pallas_call(functools.partial(fused_kernel, sizes), out_shape=(jax.Sha...  24.4 us
    pallas_call x1, Pallas kernels, fused(): pl.pallas_call(emit_kernel, out_shape=(jax.ShapeDtypeStruct(residual.shap...  0.65 us

profile of v5, /device:TPU:0, one launch (start us, length us, event | category | flops | bytes accessed | tf_op | source)
XLA Modules:
  0.0 25.7 jit_solution(17370400037882941182)
XLA Ops:
  0.6 24.4 %shard_map.167 = (f32[8,32]{1,0:T(8,128)S(1)}, f32[16,1024]{1,0:T(8,128)S(1)}) custom-call(s32[3,1,8]{2,1,0:T(1,128)} %bitcast.17, s32[1022,2,128]{2,1,0:T(2,128)} %bitcast.13, f32[256,4,512]{2,1,0:T(4,128)} %gain_hbm.1, f32[32,512]{1,0:T(8,128)} %constant.18.clone.p_hbm, f32[32,512]{1,0:T(8,128)} %constant.19.clone.q_hbm, f32[64,512]{1,0:T(8,128)} %constant.20.clone.c_hbm, ...), custom_call_target="tpu_custom_call" | custom-call | tf_op jit(solution)/shard_map/pallas_call | solution.py:1179
  25.1 0.7 %shard_map.168 = (f32[8,32]{1,0:T(8,128)}, f32[16,1024]{1,0:T(8,128)}) custom-call(f32[8,32]{1,0:T(8,128)S(1)} %get-tuple-element.6.residual_ref, f32[16,1024]{1,0:T(8,128)S(1)} %get-tuple-element.7.grad_ref), custom_call_target="tpu_custom_call" | custom-call | tf_op jit(solution)/shard_map/pallas_call | solution.py:1238

commit v6 on v5

--- a/solution.py
+++ b/solution.py
@@ -769,12 +769,10 @@
         return other, (other // owners, p, lax.rem(other, owners))
 
     barrier = pltpu.get_barrier_semaphore()
-    for d in range(1, across_total):
-        pl.semaphore_signal(barrier, inc=1, device_id=across_peer(d)[1], device_id_type=mesh_id)
-    for d in range(1, pols):
-        q = lax.rem(p + d, pols)
-        for o in range(owners):
-            pl.semaphore_signal(barrier, inc=1, device_id=(z, q, o), device_id_type=mesh_id)
+    greeted = [(pair_z, p, t), (far_z, p, t), (z, p, partner)]
+    greeted += [(z, lax.rem(p + d, pols), t) for d in range(1, pols)]
+    for peer in greeted:
+        pl.semaphore_signal(barrier, inc=1, device_id=peer, device_id_type=mesh_id)
 
     offsets = [
         (dz, dp, dt)
@@ -813,25 +811,13 @@
     loads = [
         pltpu.make_async_copy(src, dst, load_sem.at[k]) for k, (src, dst) in enumerate(pairs)
     ]
-    for copy in loads[:4]:
+    for copy in loads[4:9] + loads[:4]:
         copy.start()
     x_loads[0].start()
-    for copy in loads[4:9]:
-        copy.start()
     for copy in x_loads[1:]:
         copy.start()
     for copy in loads[9:]:
         copy.start()
-
-    for copy in loads[:4]:
-        copy.wait()
-    spread = c_ref.shape[0]
-    cosine, sine = c_ref[...], s_ref[...]
-    half = length // 2
-    for part in range(half // spread):
-        factors[part * spread : (part + 1) * spread, :] = (
-            p_ref[part : part + 1, :] * cosine + q_ref[part : part + 1, :] * sine
-        ).astype(jnp.bfloat16)
 
     for copy in loads[4:9]:
         copy.wait()
@@ -842,7 +828,7 @@
         jnp.concatenate([observed_ref[...]] * pols, axis=1),
         0.0,
     )
-    pl.semaphore_wait(barrier, across_total - 1 + (pols - 1) * owners)
+    pl.semaphore_wait(barrier, len(greeted))
     share = lambda q: pl.ds(pl.multiple_of(q * quarter, quarter), quarter)
     far_copies = [
         remote(
@@ -885,6 +871,16 @@
         for copy in near_copies[others * side : others * side + others]:
             copy.start()
 
+
+    for copy in loads[:4]:
+        copy.wait()
+    spread = c_ref.shape[0]
+    cosine, sine = c_ref[...], s_ref[...]
+    half = length // 2
+    for part in range(half // spread):
+        factors[part * spread : (part + 1) * spread, :] = (
+            p_ref[part : part + 1, :] * cosine + q_ref[part : part + 1, :] * sine
+        ).astype(jnp.bfloat16)
 
     lane = lax.broadcasted_iota(jnp.int32, (rows, 2 * MC), 1)
     sign = jnp.where(lane < MC, -1.0, 1.0)
@@ -978,8 +974,6 @@
         side_copies.append(
             remote(side.at[across], side.at[across], side_send.at[d], side_recv.at[d], peer)
         )
-    for copy in side_copies:
-        copy.start()
     forward(1)
 
     span = 2 * groups * owners * rows
@@ -1020,6 +1014,9 @@
     for pair, relay in zip(pair_copies[:-1], relay_copies[:-1]):
         pair.wait_recv()
         relay.start()
+    chip_copies[-1].wait_recv()
+    for copy in side_copies:
+        copy.start()
     for copy in near_copies[:others]:
         copy.wait_recv()
     prepare_right(far)
@@ -1028,8 +1025,9 @@
     for copy in [far_copies[2]] + near_copies[others:]:
         copy.wait_recv()
     prepare_left(far)
-    for copy in chip_copies + relay_copies:
+    for copy in chip_copies[:-1] + relay_copies:
         copy.wait()
+    chip_copies[-1].wait_send()
     for k in range(2):
         spread_v = nt_dot(got[k].reshape(span, width), right[k])
         weights = depths[k].astype(jnp.float32)

time: 25.9 us -> 25.7 us (level)
  no operation moved by 1% of the time
where the time goes in v6:
time: 25.7 us; the launch traced here: 25.5 us
  Pallas kernels  24.9 us (97%)
  between operations  0.64 us (2%)
    pallas_call x1, Pallas kernels, fused(): pl.pallas_call(functools.partial(fused_kernel, sizes), out_shape=(jax.Sha...  24.2 us
    pallas_call x1, Pallas kernels, fused(): pl.pallas_call(emit_kernel, out_shape=(jax.ShapeDtypeStruct(residual.shap...  0.65 us

profile of v6, /device:TPU:0, one launch (start us, length us, event | category | flops | bytes accessed | tf_op | source)
XLA Modules:
  0.0 25.5 jit_solution(401623911531100463)
XLA Ops:
  0.6 24.2 %shard_map.167 = (f32[8,32]{1,0:T(8,128)S(1)}, f32[16,1024]{1,0:T(8,128)S(1)}) custom-call(s32[3,1,8]{2,1,0:T(1,128)} %bitcast.17, s32[1022,2,128]{2,1,0:T(2,128)} %bitcast.13, f32[256,4,512]{2,1,0:T(4,128)} %gain_hbm.1, f32[32,512]{1,0:T(8,128)} %constant.18.clone.p_hbm, f32[32,512]{1,0:T(8,128)} %constant.19.clone.q_hbm, f32[64,512]{1,0:T(8,128)} %constant.20.clone.c_hbm, ...), custom_call_target="tpu_custom_call" | custom-call | tf_op jit(solution)/shard_map/pallas_call | solution.py:1177
  24.9 0.7 %shard_map.168 = (f32[8,32]{1,0:T(8,128)}, f32[16,1024]{1,0:T(8,128)}) custom-call(f32[8,32]{1,0:T(8,128)S(1)} %get-tuple-element.6.residual_ref, f32[16,1024]{1,0:T(8,128)S(1)} %get-tuple-element.7.grad_ref), custom_call_target="tpu_custom_call" | custom-call | tf_op jit(solution)/shard_map/pallas_call | solution.py:1236

commit v7 on v6

--- a/solution.py
+++ b/solution.py
@@ -776,7 +776,7 @@
 
     offsets = [
         (dz, dp, dt)
-        for dz in sorted(range(subgrids), key=lambda d: -min(d, subgrids - d))
+        for dz in reversed(range(subgrids))
         for dp in reversed(range(pols))
         for dt in range(owners)
     ]
@@ -1044,7 +1044,8 @@
 
     part_copies = []
     for dz, dp, dt in offsets:
-        peer = (lax.rem(z + dz, subgrids), lax.rem(p + dp, pols), lax.rem(t + dt, owners))
+        peer_z = (z, pair_z, far_z, subgrids - 1 - z)[dz]
+        peer = (peer_z, lax.rem(p + dp, pols), lax.rem(t + dt, owners))
         k = (dz * pols + dp) * owners + dt
         part_copies.append(
             remote(part_out, part_in.at[z, p, t], part_send.at[k], part_recv.at[k], peer)

time: 25.7 us -> 25.4 us (0.988)
  Pallas kernels: 24.9 us -> 24.6 us
where the time goes in v7:
time: 25.4 us; the launch traced here: 25.3 us
  Pallas kernels  24.6 us (97%)
  between operations  0.64 us (3%)
    pallas_call x1, Pallas kernels, fused(): pl.pallas_call(functools.partial(fused_kernel, sizes), out_shape=(jax.Sha...  24 us
    pallas_call x1, Pallas kernels, fused(): pl.pallas_call(emit_kernel, out_shape=(jax.ShapeDtypeStruct(residual.shap...  0.65 us

profile of v7, /device:TPU:0, one launch (start us, length us, event | category | flops | bytes accessed | tf_op | source)
XLA Modules:
  0.0 25.3 jit_solution(17430339063356717327)
XLA Ops:
  0.6 24.0 %shard_map.167 = (f32[8,32]{1,0:T(8,128)S(1)}, f32[16,1024]{1,0:T(8,128)S(1)}) custom-call(s32[3,1,8]{2,1,0:T(1,128)} %bitcast.17, s32[1022,2,128]{2,1,0:T(2,128)} %bitcast.13, f32[256,4,512]{2,1,0:T(4,128)} %gain_hbm.1, f32[32,512]{1,0:T(8,128)} %constant.18.clone.p_hbm, f32[32,512]{1,0:T(8,128)} %constant.19.clone.q_hbm, f32[64,512]{1,0:T(8,128)} %constant.20.clone.c_hbm, ...), custom_call_target="tpu_custom_call" | custom-call | tf_op jit(solution)/shard_map/pallas_call | solution.py:1178
  24.6 0.7 %shard_map.168 = (f32[8,32]{1,0:T(8,128)}, f32[16,1024]{1,0:T(8,128)}) custom-call(f32[8,32]{1,0:T(8,128)S(1)} %get-tuple-element.6.residual_ref, f32[16,1024]{1,0:T(8,128)S(1)} %get-tuple-element.7.grad_ref), custom_call_target="tpu_custom_call" | custom-call | tf_op jit(solution)/shard_map/pallas_call | solution.py:1237
